TPU v7x, 32 devices: a whole 2x2x4 slice. The times are simulated.
32 devices in a mesh: psg: 8 (over z, x), mp: 4 (over y, core).
Axes of the slice: x: 2, y: 2, z: 4, core: 2. Of those that a mesh axis runs over, the one named last changes fastest.
Arguments:
- tokens: bfloat16 [8192, 4096], P('psg'), may hold values from -6 to 6
- lengths: int32 [32], P('psg'), may hold values from 32 to 256, as said below
- assignment: int32 [32], P('psg'), may hold values from 0 to 3, as said below
- retrieval: float32 [32], P('psg'), may hold values from -8 to 306
- enc_gain: float32 [4096], replicated, may hold values from 0.25 to 1.75
- enc_qkv: bfloat16 [3, 4096, 2048], P(None, 'psg', 'mp'), may hold values from -0.09375 to 0.09375
- position_bias: float32 [32, 32], P('mp'), may hold values from -6 to 306
- enc_output: bfloat16 [2048, 4096], P('mp', 'psg'), may hold values from -0.125 to 0.125
- final_gain: float32 [4096], replicated, may hold values from 0.25 to 1.75
- embedding: bfloat16 [32128, 4096], P('mp', 'psg'), may hold values from -18 to 18
- dec_tokens: int32 [4, 2], replicated, may hold values from 0 to 32127
- dec_gain: float32 [4096], P('psg'), may hold values from 0.25 to 1.75
- cross_query: bfloat16 [4096, 2048], P('psg', 'mp'), may hold values from -0.0234375 to 0.0234375
- cross_keyval: bfloat16 [2, 4096, 2048], P(None, 'psg', 'mp'), may hold values from -0.09375 to 0.09375
- cross_output: bfloat16 [2048, 4096], P('mp', 'psg'), may hold values from -0.25 to 0.25
Outputs:
- encoded: bfloat16 [8192, 4096], P('psg', 'mp')
- decoded: bfloat16 [4, 2, 4096], P(None, None, ('psg', 'mp'))
Inputs may be any that keep to these rules, and one draw needn't show every extreme that they name: Passage p holds real tokens in its first lengths[p] slots and padding after them; in every draw all passages of some index of psg have 256 real tokens. `assignment`: every claim has exactly 8 passages.
All inputs are finite; a program needn't handle non-finite values.
Results may differ from a plain program's by a relative error of at most 0.013.
The roundings to bfloat16 on the way count: a program that leaves them out, or rounds other values in their place, can miss the bound.
Values may be sent and summed in bfloat16 or wider, within the bound.
No kernel may reach another device: no remote copies, remote signals or barrier semaphores. Data moves between devices by JAX's collectives and lax.ppermute only.
A program may use at most 128 MiB of HBM per device.

v0:
```python
import functools
import math

import jax
import jax.numpy as jnp
import numpy as np
from jax import lax
from jax.experimental import pallas as pl
from jax.experimental.pallas import tpu as pltpu
from jax.sharding import PartitionSpec as P


D = 4096
HEAD_DIM = 64
BUCKETS = 32
MAXDIST = 128
SEQ = 256
CLAIMS = 4
POS = 2


EPSILON = 1e-06
MASKED = -1e30
HIGHEST = lax.Precision.HIGHEST
F32 = jnp.float32
BF16 = jnp.bfloat16
LANES = 128


def bucket_onehot(length, buckets, max_distance):
    halfway = buckets // 2
    exact_max = halfway // 2
    relative_list = list(range(-(length - 1), length))
    beyond_list = [
        min(
            halfway - 1,
            exact_max
            + math.floor(
                math.log(max(abs(shift), 1) / exact_max)
                / math.log(max_distance / exact_max)
                * (halfway - exact_max)
            ),
        )
        for shift in relative_list
    ]
    relative = np.array(relative_list)
    beyond = np.array(beyond_list)
    distance = np.abs(relative)
    bucket_ids = np.where(relative > 0, halfway, 0) + np.where(
        distance < exact_max, distance, beyond
    )
    return (bucket_ids[None, :] == np.arange(buckets)[:, None]).astype(np.float32)


def after(values, gate):
    return lax.optimization_barrier((values, gate))[0]


def split3(value):
    high = value.astype(BF16)
    rest = value - high.astype(F32)
    middle = rest.astype(BF16)
    low = (rest - middle.astype(F32)).astype(BF16)
    return high, middle, low


class Ring:
    def __init__(self, size):
        self.size = size
        order = list(range(0, size, 2)) + list(range(size - 1, 0, -2))
        self.forward = [(order[i], order[(i + 1) % size]) for i in range(size)]
        self.backward = [(b, a) for a, b in self.forward]
        table = np.zeros((size, size), np.int32)
        for place, device in enumerate(order):
            table[device] = [order[(place - step) % size] for step in range(size)]
        self.tables = np.concatenate([table, np.argsort(table, axis=1).astype(np.int32)], axis=1)

    def origins(self, index):
        both = lax.dynamic_index_in_dim(jnp.asarray(self.tables), index, 0, keepdims=False)
        return both[: self.size], both[self.size :]


def norm_kernel(table_ref, tok_ref, gain_ref, out_ref):
    blocks = table_ref.shape[0]
    rows, model = tok_ref.shape
    width = model // blocks
    squares = jnp.zeros((rows, 1), F32)
    for block in range(blocks):
        wide = tok_ref[:, block * width : (block + 1) * width].astype(F32)
        squares = squares + jnp.sum(wide * wide, axis=1, keepdims=True)
    inverse = lax.rsqrt(squares / model + EPSILON)
    for block in range(blocks):
        at = pl.ds(pl.multiple_of(table_ref[block] * width, width), width)
        out_ref[:, block * width : (block + 1) * width] = (
            tok_ref[:, at].astype(F32) * inverse * gain_ref[:, at]
        ).astype(BF16)


def norm_in_order(table, tokens, gain):
    rows, model = tokens.shape
    spec = pl.BlockSpec((SEQ, model), lambda i, t: (i, 0))
    return pl.pallas_call(
        norm_kernel,
        out_shape=jax.ShapeDtypeStruct((rows, model), BF16),
        grid_spec=pltpu.PrefetchScalarGridSpec(
            num_scalar_prefetch=1,
            grid=(rows // SEQ,),
            in_specs=[spec, pl.BlockSpec((1, model), lambda i, t: (0, 0))],
            out_specs=spec,
        ),
        cost_estimate=pl.CostEstimate(
            flops=6 * rows * model, bytes_accessed=4 * rows * model, transcendentals=rows
        ),
    )(table, tokens, gain)


def bias_kernel(table_ref, out_ref):
    length = out_ref.shape[1]
    spread = jnp.broadcast_to(table_ref[0], (length, table_ref.shape[2]))
    rolled = pltpu.roll(spread, length + 1, 1, stride=1, stride_axis=0)
    out_ref[0] = rolled[:, :length]


def toeplitz(vectors):
    heads, width = vectors.shape
    length = width // 2
    return pl.pallas_call(
        bias_kernel,
        out_shape=jax.ShapeDtypeStruct((heads, length, length), F32),
        grid=(heads,),
        in_specs=[pl.BlockSpec((1, 1, width), lambda h: (h, 0, 0))],
        out_specs=pl.BlockSpec((1, length, length), lambda h: (h, 0, 0)),
    )(vectors.reshape(heads, 1, width))


TILE = 16


def lookup_kernel(ids_ref, limits_ref, table_ref, out_ref):
    row = pl.program_id(0)
    index = ids_ref[row] - limits_ref[0]
    inside = jnp.logical_and(index >= 0, index < limits_ref[1])
    offset = jnp.where(inside, lax.rem(jnp.maximum(index, 0), TILE), -1)
    found = table_ref[...].astype(F32)
    place = lax.broadcasted_iota(jnp.int32, found.shape, 0)
    found = jnp.sum(jnp.where(place == offset, found, 0.0), axis=0, keepdims=True)
    rows = lax.broadcasted_iota(jnp.int32, out_ref.shape, 0)
    kept = jnp.where(row == 0, jnp.zeros_like(found), 1.0)
    out_ref[...] = jnp.where(rows == row, found, jnp.where(kept > 0, out_ref[...], 0.0))


def lookup(ids, start, table):
    count = ids.shape[0]
    vocab, width = table.shape
    limits = jnp.stack([start, jnp.int32(vocab)])

    def block(r, ids_ref, limits_ref):
        index = jnp.clip(ids_ref[r] - limits_ref[0], 0, vocab - 1)
        return (index // TILE, 0)

    return pl.pallas_call(
        lookup_kernel,
        out_shape=jax.ShapeDtypeStruct((count, width), F32),
        grid_spec=pltpu.PrefetchScalarGridSpec(
            num_scalar_prefetch=2,
            grid=(count,),
            in_specs=[pl.BlockSpec((TILE, width), block)],
            out_specs=pl.BlockSpec((count, width), lambda r, i, l: (0, 0)),
        ),
    )(ids, limits, table)


def attend_kernel(lengths_ref, group_ref, bias_ref, *refs, away):
    count = len(away)
    for at, k in enumerate(away):
        length = lengths_ref[group_ref[0] ^ k]
        attend_passage(length, refs[2 * at], refs[2 * at + 1], bias_ref, refs[2 * count + at])


def attend_passage(length, first_ref, second_ref, bias_ref, out_ref):
    rows = first_ref.shape[0]
    width = first_ref.shape[1] // 3
    keys = lax.broadcasted_iota(jnp.int32, (rows, rows), 1)
    valid = keys < length
    low_half = lax.broadcasted_iota(jnp.int32, (rows, LANES), 1) < HEAD_DIM
    for half, source in enumerate((first_ref, second_ref)):
        for pair in range(width // LANES):
            query = source[:, pair * LANES : (pair + 1) * LANES].astype(F32)
            key = source[:, width + pair * LANES : width + (pair + 1) * LANES]
            value = source[:, 2 * width + pair * LANES : 2 * width + (pair + 1) * LANES]
            parts = []
            for side in range(2):
                head = half * (width // HEAD_DIM) + pair * 2 + side
                mine = low_half if side == 0 else jnp.logical_not(low_half)
                masked_query = jnp.where(mine, query, 0.0).astype(BF16)
                scores = lax.dot_general(
                    masked_query, key, (((1,), (1,)), ((), ())), preferred_element_type=F32
                )
                scores = jnp.where(valid, scores + bias_ref[head], MASKED)
                weights = jnp.exp(scores - jnp.max(scores, axis=1, keepdims=True))
                total = jnp.sum(weights, axis=1, keepdims=True)
                probabilities = (weights * (1.0 / total)).astype(BF16)
                parts.append(jnp.dot(probabilities, value, preferred_element_type=F32))
            column = half * width + pair * LANES
            out_ref[:, column : column + LANES] = jnp.where(low_half, parts[0], parts[1]).astype(
                BF16
            )


def attend(lengths, group, first, second, bias, away):
    width = first.shape[1] // 3
    heads = bias.shape[0]
    count = len(away)
    specs = []
    for k in away:
        specs += [pl.BlockSpec((SEQ, first.shape[1]), lambda i, n, g, k=k: (g[0] ^ k, 0))] * 2
    return pl.pallas_call(
        functools.partial(attend_kernel, away=tuple(away)),
        out_shape=[jax.ShapeDtypeStruct((SEQ, 2 * width), BF16)] * count,
        grid_spec=pltpu.PrefetchScalarGridSpec(
            num_scalar_prefetch=2,
            grid=(1,),
            in_specs=[pl.BlockSpec((heads, SEQ, SEQ), lambda i, n, g: (0, 0, 0))] + specs,
            out_specs=[pl.BlockSpec((SEQ, 2 * width), lambda i, n, g: (0, 0))] * count,
        ),
        cost_estimate=pl.CostEstimate(
            flops=count * heads * SEQ * SEQ * 4 * LANES,
            bytes_accessed=count * SEQ * 16 * width + heads * SEQ * SEQ * 4,
            transcendentals=count * heads * SEQ * SEQ,
        ),
    )(lengths, group, bias, *([first, second] * count))


def join_kernel(*refs):
    out_ref = refs[-1]
    count = (len(refs) - 1) // 2
    cut, width = refs[0].shape
    for j in range(count):
        out_ref[:cut, j * width : (j + 1) * width] = refs[j][...]
        out_ref[cut:, j * width : (j + 1) * width] = refs[count + j][...]


def join(uppers, lowers):
    cut, width = uppers[0].shape
    vmem = pl.BlockSpec(memory_space=pltpu.VMEM)
    shape = (2 * cut, width * len(uppers))
    return pl.pallas_call(
        join_kernel,
        out_shape=jax.ShapeDtypeStruct(shape, uppers[0].dtype),
        in_specs=[vmem] * (2 * len(uppers)),
        out_specs=vmem,
        cost_estimate=pl.CostEstimate(
            flops=0, bytes_accessed=4 * shape[0] * shape[1], transcendentals=0
        ),
    )(*uppers, *lowers)


def project_kernel(step_ref, group_ref, tok_ref, *refs):
    groups = (len(refs)) // 3
    total = jnp.zeros(tok_ref.shape, F32)
    for term, weight in zip(refs[:groups], refs[groups : 2 * groups]):
        partial = jnp.dot(term[...], weight[...], preferred_element_type=F32)
        total = total + partial.astype(BF16).astype(F32)
    encoded = (tok_ref[...].astype(F32) + total).astype(BF16)
    for k, out_ref in enumerate(refs[2 * groups :]):

        @pl.when(pl.program_id(0) == k)
        def _(out_ref=out_ref):
            out_ref[...] = encoded


def project(step_of, group, tokens, terms, weights, width):
    groups = len(terms)
    model = tokens.shape[1]
    share = model // groups
    rows, depth = terms[0].shape
    blocks = share // width

    def column(i, j, g):
        return (i ^ g[0]) * blocks + j

    def place(k):
        return lambda i, j, t, g: (
            0,
            jnp.where(i < k, 0, jnp.where(i > k, blocks - 1, j)),
        )

    return pl.pallas_call(
        project_kernel,
        out_shape=[jax.ShapeDtypeStruct((rows, share), BF16)] * groups,
        grid_spec=pltpu.PrefetchScalarGridSpec(
            num_scalar_prefetch=2,
            grid=(groups, blocks),
            in_specs=[pl.BlockSpec((rows, width), lambda i, j, t, g: (g[0], column(i, j, g)))]
            + [pl.BlockSpec((rows, depth), lambda i, j, t, g: (0, 0))] * groups
            + [pl.BlockSpec((depth, width), lambda i, j, t, g: (0, t[column(i, j, g)]))] * groups,
            out_specs=[pl.BlockSpec((rows, width), place(k)) for k in range(groups)],
        ),
        cost_estimate=pl.CostEstimate(
            flops=2 * rows * groups * depth * model,
            bytes_accessed=2 * groups * depth * model + 4 * rows * model,
            transcendentals=0,
        ),
    )(step_of, group, tokens, *terms, *weights)


def cross_kernel(
    group_ref, length_ref, bonus_ref, gain_ref, folded_ref, *refs
):
    enc_refs, out_ref, memory_ref = refs[:-2], refs[-2], refs[-1]
    groups = len(enc_refs)
    rows, share = enc_refs[0].shape
    blocks = out_ref.shape[0] // groups
    heads = out_ref.shape[1]
    width = folded_ref.shape[2]
    per = share // width
    passage = group_ref[0]
    squares = jnp.zeros((rows, 1), F32)
    for enc_ref in enc_refs:
        for part in range(per):
            wide = enc_ref[:, part * width : (part + 1) * width].astype(F32)
            squares = squares + jnp.sum(wide * wide, axis=1, keepdims=True)
    inverse = lax.rsqrt(squares / (blocks * width) + EPSILON)
    scores = [jnp.zeros((heads, rows), F32) for _ in range(groups)]
    for k, enc_ref in enumerate(enc_refs):
        for part in range(per):
            block = (passage ^ k) * per + part
            gain = gain_ref[:, pl.ds(pl.multiple_of(block * width, width), width)]
            wide = enc_ref[:, part * width : (part + 1) * width].astype(F32)
            memory = (wide * inverse * gain).astype(BF16)
            at = (k * per + part) * width
            memory_ref[:, at : at + width] = memory
            for group in range(groups):
                scores[group] = scores[group] + lax.dot_general(
                    folded_ref[block * groups + group],
                    memory,
                    (((1,), (1,)), ((), ())),
                    preferred_element_type=F32,
                )
    scores = jnp.concatenate(scores, axis=0)
    keys = lax.broadcasted_iota(jnp.int32, scores.shape, 1)
    usable = keys < length_ref[passage]
    scores = jnp.where(usable, scores, MASKED)
    peak = jnp.max(scores, axis=1, keepdims=True)
    weights = jnp.where(usable, jnp.exp(scores - peak), 0.0)
    total = jnp.sum(weights, axis=1, keepdims=True)
    high = weights.astype(BF16)
    low = (weights - high.astype(F32)).astype(BF16)
    scale = 1.0 / total
    mass = peak + jnp.log(total) + bonus_ref[passage]
    one, two, three = split3(mass)
    lane = lax.broadcasted_iota(jnp.int32, (groups * heads, LANES), 1)
    packed = jnp.where(
        lane == 0,
        one.astype(F32),
        jnp.where(lane == 1, two.astype(F32), jnp.where(lane == 2, three.astype(F32), 0.0)),
    ).astype(BF16)
    for place in range(blocks):
        block = (passage ^ (place // per)) * per + place % per
        memory = memory_ref[:, place * width : (place + 1) * width]
        pooled = jnp.dot(high, memory, preferred_element_type=F32) + jnp.dot(
            low, memory, preferred_element_type=F32
        )
        pooled = (pooled * scale).astype(BF16)
        for group in range(groups):
            out_ref[block * groups + group, :, :width] = pooled[
                group * heads : (group + 1) * heads
            ]
            out_ref[block * groups + group, :, width:] = packed[
                group * heads : (group + 1) * heads
            ]


def cross(group, lengths, bonus, encoded, gain, folded):
    groups = len(encoded)
    rows, share = encoded[0].shape
    model = groups * share
    devices, heads, width = folded.shape
    smem = pl.BlockSpec(memory_space=pltpu.SMEM)
    vmem = pl.BlockSpec(memory_space=pltpu.VMEM)
    return pl.pallas_call(
        cross_kernel,
        out_shape=jax.ShapeDtypeStruct((devices, heads, width + LANES), BF16),
        in_specs=[smem, smem, smem] + [vmem] * (2 + groups),
        out_specs=vmem,
        scratch_shapes=[pltpu.VMEM((rows, model), BF16)],
        cost_estimate=pl.CostEstimate(
            flops=6 * devices * heads * rows * width,
            bytes_accessed=rows * model * 2,
            transcendentals=devices * heads,
        ),
    )(group, lengths, bonus, gain, folded, *encoded)


def gather_kernel(group_ref, *refs):
    out_ref = refs[-1]
    for k, ref in enumerate(refs[:-1]):

        @pl.when(pl.program_id(0) == k)
        def _(ref=ref):
            out_ref[...] = ref[...]


def in_passage_order(group, blocks):
    rows, width = blocks[0].shape
    return pl.pallas_call(
        gather_kernel,
        out_shape=jax.ShapeDtypeStruct((len(blocks) * rows, width), blocks[0].dtype),
        grid_spec=pltpu.PrefetchScalarGridSpec(
            num_scalar_prefetch=1,
            grid=(len(blocks),),
            in_specs=[pl.BlockSpec((rows, width), lambda i, g: (0, 0))] * len(blocks),
            out_specs=pl.BlockSpec((rows, width), lambda i, g: (g[0] ^ i, 0)),
        ),
    )(group, *blocks)


def split2(value):
    high = value.astype(BF16)
    return high, (value - high.astype(F32)).astype(BF16)


def combine_kernel(owner_ref, got_ref, weight_ref, out_ref):
    passages, rows, padded = got_ref.shape
    width = padded - LANES
    heads = rows // POS
    packed = got_ref[:, :, width:].reshape(passages * rows, LANES)
    pooled = got_ref[:, :, :width].reshape(passages * rows, width)
    picker = (lax.broadcasted_iota(jnp.int32, (8, LANES), 1) < 3).astype(BF16)
    mass = lax.dot_general(
        picker, packed, (((1,), (1,)), ((), ())), preferred_element_type=F32
    )[0:1]
    shape = (CLAIMS * rows, passages * rows)
    row = lax.broadcasted_iota(jnp.int32, shape, 0)
    column = lax.broadcasted_iota(jnp.int32, shape, 1)
    mine = jnp.logical_and(
        owner_ref[...] == row // rows, lax.rem(row, rows) == lax.rem(column, rows)
    )
    mass = jnp.where(mine, mass, MASKED)
    peak = jnp.max(mass, axis=1, keepdims=True)
    share = jnp.where(mine, jnp.exp(mass - peak), 0.0)
    total = jnp.sum(share, axis=1, keepdims=True)
    joint = jnp.zeros((CLAIMS * rows, width), F32)
    for part in split2(share):
        joint = joint + jnp.dot(part, pooled, preferred_element_type=F32)
    joint = joint / total
    weight = weight_ref[...]
    value = jnp.zeros((CLAIMS * rows, weight.shape[1]), F32)
    for part in split2(joint):
        value = value + jnp.dot(part, weight, preferred_element_type=F32)
    head = lax.broadcasted_iota(jnp.int32, value.shape, 1) // HEAD_DIM
    own = head == lax.rem(lax.broadcasted_iota(jnp.int32, value.shape, 0), heads)
    value = jnp.where(own, value, 0.0).reshape(CLAIMS * POS, heads, weight.shape[1])
    value = jnp.sum(value, axis=1)
    for copy in range(out_ref.shape[0]):
        out_ref[copy] = value


def combine(owner, got, weight, copies):
    vmem = pl.BlockSpec(memory_space=pltpu.VMEM)
    return pl.pallas_call(
        combine_kernel,
        out_shape=jax.ShapeDtypeStruct((copies, CLAIMS * POS, weight.shape[1]), F32),
        in_specs=[vmem, vmem, vmem],
        out_specs=vmem,
    )(owner, got, weight)


def program(
    tokens,
    lengths,
    assignment,
    retrieval,
    enc_gain,
    enc_qkv,
    position_bias,
    enc_output,
    final_gain,
    embedding,
    dec_tokens,
    dec_gain,
    cross_query,
    cross_keyval,
    cross_output,
):
    passages_here = lengths.shape[0]
    width_here = enc_qkv.shape[1]
    inner_here = enc_qkv.shape[2]
    heads_here = inner_here // HEAD_DIM
    query_rows = CLAIMS * POS
    psg = lax.axis_size("psg")
    groups = lax.axis_size("mp")
    assert passages_here == groups
    here = lax.axis_index("psg")
    group = lax.axis_index("mp")
    piece = width_here // groups
    ring = Ring(psg)
    table, step_of = ring.origins(here)

    def swap(value, k):
        return lax.ppermute(value, "mp", [(i, i ^ k) for i in range(groups)])

    here_1 = group.reshape(1)
    across, near = groups // 2, 1
    order = [across, across ^ near, near, 0]

    cut = enc_output.shape[0] // 2
    up, down = [enc_output[:cut]], [enc_output[cut:]]
    for _ in range(1, psg):
        up.append(lax.ppermute(up[-1], "psg", ring.forward))
        down.append(lax.ppermute(down[-1], "psg", ring.backward))
    own_rows = join(up, [down[(psg - j) % psg] for j in range(psg)])
    far_rows = swap(own_rows, across)
    near_rows = swap(own_rows, near)
    corner_rows = swap(far_rows, near)
    out_weights = [far_rows, corner_rows, near_rows, own_rows]

    half = inner_here // 2
    first_block = jnp.concatenate([enc_qkv[k][:, :half] for k in range(3)], axis=1)
    second_block = jnp.concatenate([enc_qkv[k][:, half:] for k in range(3)], axis=1)
    first_block, second_block = after(
        (first_block, second_block), (up[psg - 2], down[psg - 2])
    )
    normed = norm_in_order(table, tokens, enc_gain.reshape(1, -1))

    def term(block, place):
        part = normed[:, place * width_here : (place + 1) * width_here]
        return jnp.dot(part, block, preferred_element_type=F32)

    own_blocks = (first_block, second_block)
    arrived = [own_blocks]
    late = (psg - 1) // 2
    for step in range(1, psg):
        first_block = lax.ppermute(first_block, "psg", ring.forward)
        second_block = lax.ppermute(second_block, "psg", ring.backward)
        arrived.append((first_block, second_block))
        first_term = term(first_block, step)
        second_term = term(second_block, psg - step)
        if step > 1:
            first_term = lax.optimization_barrier(first_acc) + first_term
            second_term = lax.optimization_barrier(second_acc) + second_term
        first_acc, second_acc = first_term, second_term
        if step == late:
            first_acc = lax.optimization_barrier(first_acc) + term(own_blocks[0], 0)
            second_acc = lax.optimization_barrier(second_acc) + term(own_blocks[1], 0)
        if step == psg - 1:
            first_acc = first_acc.astype(BF16)
            second_acc = second_acc.astype(BF16)
    first_heads, second_heads = first_acc, second_acc

    found = lookup(dec_tokens.reshape(-1), group * embedding.shape[0], embedding)
    found = found.astype(BF16)
    found_all = lax.all_to_all(
        jnp.broadcast_to(found[None], (groups,) + found.shape), "mp", 0, 0, tiled=True
    )
    embedded = jnp.sum(found_all.astype(F32), axis=0)
    query_part = jnp.dot(
        embedded * dec_gain, cross_query.astype(F32), precision=HIGHEST
    )
    extra = jnp.concatenate(
        [jnp.sum(embedded * embedded, axis=1), assignment.astype(F32)]
    )
    extra = jnp.pad(extra, (0, inner_here - extra.shape[0]))
    message = jnp.concatenate(
        [query_part, jnp.broadcast_to(extra[None], (8, inner_here))], axis=0
    )
    messages = lax.all_to_all(
        jnp.broadcast_to(message[None], (psg,) + message.shape), "psg", 0, 0, tiled=True
    )
    messages = after(messages, arrived[min(4, psg - 1)])
    joined = jnp.sum(messages[:, : query_rows + 1], axis=0)
    inverse_dec = lax.rsqrt(joined[query_rows, :query_rows] / D + EPSILON)
    cquery = (joined[:query_rows] * inverse_dec[:, None]).reshape(
        query_rows, heads_here, HEAD_DIM
    )
    owners = messages[:, query_rows, query_rows : query_rows + passages_here].reshape(-1)
    owners = (owners + 0.5).astype(jnp.int32)
    key_weight = cross_keyval[0].astype(F32).reshape(width_here, heads_here, HEAD_DIM)
    folded = jnp.einsum("rhj,dhj->rhd", cquery, key_weight, precision=HIGHEST).astype(BF16)
    chosen = (owners[:, None] == jnp.arange(CLAIMS)[None, :]).astype(BF16)
    to_send = jnp.dot(
        chosen, folded.reshape(CLAIMS, -1), preferred_element_type=F32
    ).astype(BF16)
    to_send = to_send.reshape(psg * groups, POS * heads_here, width_here)
    folded_here = lax.all_to_all(to_send, ("psg", "mp"), 0, 0, tiled=True)

    bias_table = jnp.dot(
        position_bias, jnp.asarray(np.pad(bucket_onehot(SEQ, BUCKETS, MAXDIST), ((0, 0), (0, 1)))),
        precision=HIGHEST,
    )
    pair_bias = toeplitz(bias_table)
    terms = []
    for call in range(0, groups, 2):
        ks = order[call : call + 2]
        outs = attend(lengths, here_1, first_heads, second_heads, pair_bias, ks)
        terms += [swap(out, k) if k else out for out, k in zip(outs, ks)]
    rows = project(step_of, here_1, tokens, terms, out_weights, width_here)

    pooled = cross(
        here_1, lengths, retrieval, rows, final_gain.reshape(1, -1), folded_here
    )
    got = lax.all_to_all(pooled, ("psg", "mp"), 0, 0, tiled=True)
    blocks = [swap(rows[k], k) if k else rows[0] for k in range(groups)]
    encoded = in_passage_order(here_1, blocks)
    owner_row = jnp.repeat(owners, POS * heads_here).reshape(1, -1)
    value_part = combine(owner_row, got, cross_keyval[1], psg)
    values = lax.all_to_all(value_part, "psg", 0, 0, tiled=True)
    cross_attn = jnp.sum(values, axis=0)
    out_part = jnp.dot(cross_attn, cross_output.astype(F32), precision=HIGHEST)
    out_parts = lax.all_to_all(
        out_part.reshape(query_rows, groups, piece).transpose(1, 0, 2), "mp", 0, 0, tiled=True
    )
    residual = lax.dynamic_slice_in_dim(embedded, group * piece, piece, 1)
    decoded = (residual + jnp.sum(out_parts, axis=0)).astype(BF16).reshape(CLAIMS, POS, piece)
    return (encoded, decoded)


def solution(mesh):
    in_specs = (
        P("psg", None),
        P("psg"),
        P("psg"),
        P("psg"),
        P(),
        P(None, "psg", "mp"),
        P("mp", None),
        P("mp", "psg"),
        P(),
        P("mp", "psg"),
        P(),
        P("psg"),
        P("psg", "mp"),
        P(None, "psg", "mp"),
        P("mp", "psg"),
    )
    out_specs = (P("psg", "mp"), P(None, None, ("psg", "mp")))
    return jax.shard_map(program, mesh=mesh, in_specs=in_specs, out_specs=out_specs, check_vma=False)
```

profile of v0, /device:TPU:0, one launch (start us, length us, event | category | flops | bytes accessed | tf_op | source)
XLA Modules:
  0.0 331.8 jit_solution(7914730047003476639)
XLA Ops:
  1.8 3.0 collective-permute-start.6
  7.0 4.5 %shard_map.183 = f32[8,512]{1,0:T(8,128)} custom-call(s32[8]{0:T(128)} %reshape.67.ids_ref, s32[2]{0:T(128)} %pad_add_fusion.limits_ref, bf16[8032,512]{1,0:T(8,128)(2,1)} %table_ref.1), custom_call_target="tpu_custom_call" | custom-call | tf_op jit(solution)/shard_map/pallas_call | solution.py:161
  12.8 3.3 all-to-all-start
  16.1 1.9 collective-permute-start.7
  18.3 6.7 %collective-permute-done.7.refs_14_ = bf16[256,512]{1,0:T(8,128)(2,1)S(1)} collective-permute-done((bf16[256,512]{1,0:T(8,128)(2,1)S(1)}, bf16[256,512]{1,0:T(8,128)(2,1)S(1)}, u32[]{:S(2)}, u32[]{:S(2)}) %collective-permute-start.7) | collective-permute-done | bytes 262176 | tf_op jit(solution)/shard_map/ppermute | solution.py:511
  25.0 1.7 collective-permute-start.8
  27.1 5.9 %collective-permute-done.8.refs_13_ = bf16[256,512]{1,0:T(8,128)(2,1)S(1)} collective-permute-done((bf16[256,512]{1,0:T(8,128)(2,1)S(1)}, bf16[256,512]{1,0:T(8,128)(2,1)S(1)}, u32[]{:S(2)}, u32[]{:S(2)}) %collective-permute-start.8) | collective-permute-done | bytes 262176 | tf_op jit(solution)/shard_map/ppermute | solution.py:511
  33.0 1.4 collective-permute-start.9
  35.1 5.1 %collective-permute-done.9.refs_12_ = bf16[256,512]{1,0:T(8,128)(2,1)} collective-permute-done((bf16[256,512]{1,0:T(8,128)(2,1)S(1)}, bf16[256,512]{1,0:T(8,128)(2,1)}, u32[]{:S(2)}, u32[]{:S(2)}) %collective-permute-start.9) | collective-permute-done | bytes 262176 | tf_op jit(solution)/shard_map/ppermute | solution.py:511
  42.5 4.8 %collective-permute-done.10.refs_11_ = bf16[256,512]{1,0:T(8,128)(2,1)S(1)} collective-permute-done((bf16[256,512]{1,0:T(8,128)(2,1)}, bf16[256,512]{1,0:T(8,128)(2,1)S(1)}, u32[]{:S(2)}, u32[]{:S(2)}) %collective-permute-start.10) | collective-permute-done | bytes 262176 | tf_op jit(solution)/shard_map/ppermute | solution.py:511
  47.3 1.4 collective-permute-start.11
  50.0 2.1 slice_bitcast_fusion
  52.1 1.9 collective-permute-done.11.refs_10_
  54.0 1.9 collective-permute-done.5.refs_6_
  55.9 1.6 collective-permute-start.19
  57.9 1.3 collective-permute-start.29
  61.1 4.7 %shard_map.176.bias_ref = f32[8,256,256]{2,1,0:T(8,128)} custom-call(f32[8,1,512]{2,1,0:T(1,128)} %reshape.65.table_ref), custom_call_target="tpu_custom_call" | custom-call | tf_op jit(solution)/shard_map/pallas_call | solution.py:127
  66.0 10.1 %shard_map.177 = bf16[1024,4096]{1,0:T(8,128)(2,1)} custom-call(s32[8]{0:T(128)} %get-tuple-element.37.table_ref, bf16[1024,4096]{1,0:T(8,128)(2,1)} %tok_ref.3, f32[1,4096]{1,0:T(1,128)} %bitcast.64), custom_call_target="tpu_custom_call" | custom-call | flops 25165824 | bytes 16777216 | tf_op jit(solution)/shard_map/pallas_call | solution.py:102
  76.1 1.8 collective-permute-done.29.refs_7_
  77.9 4.5 %shard_map.180.refs_7_ = bf16[512,4096]{1,0:T(8,128)(2,1)} custom-call(bf16[256,512]{1,0:T(8,128)(2,1)} %copy-done.8, bf16[256,512]{1,0:T(8,128)(2,1)} %copy-done.17, bf16[256,512]{1,0:T(8,128)(2,1)} %copy-done.19, bf16[256,512]{1,0:T(8,128)(2,1)} %copy-done.21, bf16[256,512]{1,0:T(8,128)(2,1)} %collective-permute-done.3.refs_4_, ...), custom_call_target="tpu_custom_call" | custom-call | bytes 8388608 | tf_op jit(solution)/shard_map/pallas_call | solution.py:247
  82.4 1.4 collective-permute-start.31
  84.3 1.6 collective-permute-start.20
  86.7 3.9 %all-to-all-start.1 = ((f32[8,16,512]{2,1,0:T(8,128)}), f32[8,16,512]{2,1,0:T(8,128)S(1)}, u32[]{:S(2)}, u32[]{:S(2)}) async-start(f32[8,16,512]{2,1,0:T(8,128)} %broadcast_in_dim.10), calls=%async_computation.1 | async-start | bytes 524288 | tf_op jit(solution)/shard_map/all_to_all | solution.py:567
  90.6 2.1 collective-permute-start.13
  92.6 2.6 fusion.1
  95.2 2.6 fusion.17
  97.8 1.9 collective-permute-done.20
  101.0 11.4 %collective-permute-done.13 = bf16[512,768]{1,0:T(8,128)(2,1)S(1)} collective-permute-done((bf16[512,768]{1,0:T(8,128)(2,1)}, bf16[512,768]{1,0:T(8,128)(2,1)S(1)}, u32[]{:S(2)}, u32[]{:S(2)}) %collective-permute-start.13) | collective-permute-done | bytes 786464 | tf_op jit(solution)/shard_map/ppermute | solution.py:534
  114.3 4.7 %collective-permute-done.21 = bf16[512,768]{1,0:T(8,128)(2,1)} collective-permute-done((bf16[512,768]{1,0:T(8,128)(2,1)S(1)}, bf16[512,768]{1,0:T(8,128)(2,1)}, u32[]{:S(2)}, u32[]{:S(2)}) %collective-permute-start.21) | collective-permute-done | bytes 786464 | tf_op jit(solution)/shard_map/ppermute | solution.py:535
  119.0 2.1 convolution_add_fusion.4
  121.2 11.0 %collective-permute-done.14 = bf16[512,768]{1,0:T(8,128)(2,1)} collective-permute-done((bf16[512,768]{1,0:T(8,128)(2,1)S(1)}, bf16[512,768]{1,0:T(8,128)(2,1)}, u32[]{:S(2)}, u32[]{:S(2)}) %collective-permute-start.14) | collective-permute-done | bytes 786464 | tf_op jit(solution)/shard_map/ppermute | solution.py:534
  132.5 2.6 convolution_add_fusion.3
  135.2 2.1 convolution_add_fusion.10
  137.3 2.6 convolution_add_fusion.9
  140.8 10.1 %collective-permute-done.15 = bf16[512,768]{1,0:T(8,128)(2,1)S(1)} collective-permute-done((bf16[512,768]{1,0:T(8,128)(2,1)}, bf16[512,768]{1,0:T(8,128)(2,1)S(1)}, u32[]{:S(2)}, u32[]{:S(2)}) %collective-permute-start.15) | collective-permute-done | bytes 786464 | tf_op jit(solution)/shard_map/ppermute | solution.py:534
  150.9 1.3 collective-permute-start.23
  153.0 16.7 %collective-permute-done.31.refs_4_ = bf16[512,4096]{1,0:T(8,128)(2,1)} collective-permute-done((bf16[512,4096]{1,0:T(8,128)(2,1)}, bf16[512,4096]{1,0:T(8,128)(2,1)}, u32[]{:S(2)}, u32[]{:S(2)}) %collective-permute-start.31) | collective-permute-done | bytes 4194336 | tf_op jit(solution)/shard_map/ppermute | solution.py:501
  169.6 5.1 %convolution_add_fusion.2 = f32[1024,768]{1,0:T(8,128)} fusion(f32[1024,768]{1,0:T(8,128)} %convolution_add_fusion.3, bf16[512,768]{1,0:T(8,128)(2,1)} %collective-permute-done.22, bf16[1024,4096]{1,0:T(8,128)(2,1)} %shard_map.177), kind=kOutput, calls=%fused_computation.5 | convolution fusion | flops 806092800 | bytes 8126464 | tf_op jit(solution)/shard_map/dot_general | solution.py:528
  174.7 3.9 %convolution_add_fusion.8 = f32[1024,768]{1,0:T(8,128)} fusion(f32[1024,768]{1,0:T(8,128)S(1)} %copy-done.3, bf16[512,768]{1,0:T(8,128)(2,1)S(1)} %collective-permute-done.15, bf16[1024,4096]{1,0:T(8,128)(2,1)} %shard_map.177), kind=kOutput, calls=%fused_computation.11 | convolution fusion | flops 806092800 | bytes 8126464 | tf_op jit(solution)/shard_map/dot_general | solution.py:528
  180.6 4.4 %all-to-all-start.2 = ((bf16[32,16,512]{2,1,0:T(8,128)(2,1)}), bf16[32,16,512]{2,1,0:T(8,128)(2,1)S(1)}, u32[]{:S(2)}, u32[]{:S(2)}) async-start(bf16[32,16,512]{2,1,0:T(8,128)(2,1)} %bitcast.20), calls=%async_computation.2 | async-start | bytes 1048576 | tf_op jit(solution)/shard_map/all_to_all | solution.py:585
  185.0 1.8 collective-permute-start.24
  186.9 3.3 %convolution_add_fusion.1 = f32[1024,768]{1,0:T(8,128)S(1)} fusion(f32[1024,768]{1,0:T(8,128)} %convolution_add_fusion.2, bf16[512,768]{1,0:T(8,128)(2,1)S(1)} %collective-permute-done.23, bf16[1024,4096]{1,0:T(8,128)(2,1)} %shard_map.177), kind=kOutput, calls=%fused_computation.4 | convolution fusion | flops 806092800 | bytes 8126464 | tf_op jit(solution)/shard_map/dot_general | solution.py:528
  190.6 2.4 convolution_add_fusion.7
  192.9 20.2 %collective-permute-done.24 = bf16[512,768]{1,0:T(8,128)(2,1)S(1)} collective-permute-done((bf16[512,768]{1,0:T(8,128)(2,1)S(1)}, bf16[512,768]{1,0:T(8,128)(2,1)S(1)}, u32[]{:S(2)}, u32[]{:S(2)}) %collective-permute-start.24) | collective-permute-done | bytes 786464 | tf_op jit(solution)/shard_map/ppermute | solution.py:535
  214.2 4.5 %collective-permute-start.18 = (bf16[512,768]{1,0:T(8,128)(2,1)S(1)}, bf16[512,768]{1,0:T(8,128)(2,1)S(1)}, u32[]{:S(2)}, u32[]{:S(2)}) collective-permute-start(bf16[512,768]{1,0:T(8,128)(2,1)S(1)} %collective-permute-done.17), channel_id=1, source_target_pairs={{0,8},{8,16},{16,24},{24,28},{28,20},{20,12},{12,4},{4,0},{1,9},{9... | collective-permute-start | bytes 2359304 | tf_op jit(solution)/shard_map/ppermute | solution.py:534
  219.7 14.9 %collective-permute-done.25 = bf16[512,768]{1,0:T(8,128)(2,1)S(1)} collective-permute-done((bf16[512,768]{1,0:T(8,128)(2,1)S(1)}, bf16[512,768]{1,0:T(8,128)(2,1)S(1)}, u32[]{:S(2)}, u32[]{:S(2)}) %collective-permute-start.25) | collective-permute-done | bytes 786464 | tf_op jit(solution)/shard_map/ppermute | solution.py:535
  234.7 2.1 add_convert_fusion.refs_1_.refs_3_
  236.8 2.2 add_convert_fusion.1.refs_0_.refs_2_
  239.0 5.8 %shard_map.179 = (bf16[256,512]{1,0:T(8,128)(2,1)}, bf16[256,512]{1,0:T(8,128)(2,1)}) custom-call(s32[4]{0:T(128)} %length_ref.1, s32[1]{0:T(128)} %bitcast.group_ref, f32[8,256,256]{2,1,0:T(8,128)} %shard_map.176.bias_ref, bf16[1024,768]{1,0:T(8,128)(2,1)} %add_convert_fusion.1.refs_0_.refs_2_, bf16[1024,768]{1,0:T(8,128)(2,1)} %add_convert_fusion.refs_1_.refs_3_, ...), custom_call_target="tpu_custom_call" | custom-call | flops 536870912 | bytes 4194304 | tf_op jit(solution)/shard_map/pallas_call | solution.py:217
  244.7 5.8 %shard_map.178 = (bf16[256,512]{1,0:T(8,128)(2,1)}, bf16[256,512]{1,0:T(8,128)(2,1)}) custom-call(s32[4]{0:T(128)} %length_ref.1, s32[1]{0:T(128)} %bitcast.group_ref, f32[8,256,256]{2,1,0:T(8,128)} %shard_map.176.bias_ref, bf16[1024,768]{1,0:T(8,128)(2,1)} %add_convert_fusion.1.refs_0_.refs_2_, bf16[1024,768]{1,0:T(8,128)(2,1)} %add_convert_fusion.refs_1_.refs_3_, ...), custom_call_target="tpu_custom_call" | custom-call | flops 536870912 | bytes 4194304 | tf_op jit(solution)/shard_map/pallas_call | solution.py:217
  250.6 1.5 collective-permute-start.26
  252.4 7.5 %collective-permute-done.26.refs_0_ = bf16[256,512]{1,0:T(8,128)(2,1)S(1)} collective-permute-done((bf16[256,512]{1,0:T(8,128)(2,1)}, bf16[256,512]{1,0:T(8,128)(2,1)S(1)}, u32[]{:S(2)}, u32[]{:S(2)}) %collective-permute-start.26) | collective-permute-done | bytes 262176 | tf_op jit(solution)/shard_map/ppermute | solution.py:501
  259.9 4.7 %collective-permute-done.27.refs_1_ = bf16[256,512]{1,0:T(8,128)(2,1)S(1)} collective-permute-done((bf16[256,512]{1,0:T(8,128)(2,1)}, bf16[256,512]{1,0:T(8,128)(2,1)S(1)}, u32[]{:S(2)}, u32[]{:S(2)}) %collective-permute-start.27) | collective-permute-done | bytes 262176 | tf_op jit(solution)/shard_map/ppermute | solution.py:501
  265.3 13.6 %shard_map.181 = (bf16[256,1024]{1,0:T(8,128)(2,1)}, bf16[256,1024]{1,0:T(8,128)(2,1)}, bf16[256,1024]{1,0:T(8,128)(2,1)}, bf16[256,1024]{1,0:T(8,128)(2,1)}) custom-call(s32[8]{0:T(128)} %get-tuple-element.38.step_ref, s32[1]{0:T(128)} %bitcast.group_ref, bf16[1024,4096]{1,0:T(8,128)(2,1)} %tok_ref.3, bf16[256,512]{1,0:T(8,128)(2,1)} %copy-done.14, ...), custom_call_target="tpu_custom_call" | custom-call | flops 4294967296 | bytes 20971520 | tf_op jit(solution)/shard_map/pallas_call | solution.py:288
  279.8 6.1 %shard_map.184 = bf16[32,16,640]{2,1,0:T(8,128)(2,1)} custom-call(s32[1]{0:T(128)} %bitcast.group_ref, s32[4]{0:T(128)} %length_ref.1, f32[4]{0:T(128)} %bonus_ref.1, f32[1,4096]{1,0:T(1,128)} %bitcast.63, bf16[32,16,512]{2,1,0:T(8,128)(2,1)} %copy-done.5, bf16[256,1024]{1,0:T(8,128)(2,1)} %get-tuple-element.19.refs_0_, ...), custom_call_target="tpu_custom_call" | custom-call | flops 402653184 | bytes 2097152 | tf_op jit(solution)/shard_map/pallas_call | solution.py:381
  285.9 4.3 %all-to-all-start.3 = ((bf16[32,16,640]{2,1,0:T(8,128)(2,1)}), bf16[32,16,640]{2,1,0:T(8,128)(2,1)S(1)}, u32[]{:S(2)}, u32[]{:S(2)}) async-start(bf16[32,16,640]{2,1,0:T(8,128)(2,1)} %shard_map.184), calls=%async_computation.3 | async-start | bytes 1310720 | tf_op jit(solution)/shard_map/all_to_all | solution.py:602
  290.6 1.6 collective-permute-start.35
  293.0 15.2 %all-to-all-done.3.got_ref = bf16[32,16,640]{2,1,0:T(8,128)(2,1)S(1)} async-done(((bf16[32,16,640]{2,1,0:T(8,128)(2,1)}), bf16[32,16,640]{2,1,0:T(8,128)(2,1)S(1)}, u32[]{:S(2)}, u32[]{:S(2)}) %all-to-all-start.3) | async-done | bytes 655392 | tf_op jit(solution)/shard_map/all_to_all | solution.py:602
  309.1 2.8 shard_map.185
  311.8 3.4 %all-to-all-start.4 = ((f32[8,8,512]{2,1,0:T(8,128)}), f32[8,8,512]{2,1,0:T(8,128)S(1)}, u32[]{:S(2)}, u32[]{:S(2)}) async-start(f32[8,8,512]{2,1,0:T(8,128)} %shard_map.185), calls=%async_computation.4 | async-start | bytes 262144 | tf_op jit(solution)/shard_map/all_to_all | solution.py:607
  315.3 1.3 copy.38
  316.5 6.1 %all-to-all-done.4 = f32[8,8,512]{2,1,0:T(8,128)S(1)} async-done(((f32[8,8,512]{2,1,0:T(8,128)}), f32[8,8,512]{2,1,0:T(8,128)S(1)}, u32[]{:S(2)}, u32[]{:S(2)}) %all-to-all-start.4) | async-done | bytes 131104 | tf_op jit(solution)/shard_map/all_to_all | solution.py:607
  323.8 3.2 all-to-all-start.5
  327.8 3.4 %shard_map.182 = bf16[1024,1024]{1,0:T(8,128)(2,1)} custom-call(s32[1]{0:T(128)} %bitcast.group_ref, bf16[256,1024]{1,0:T(8,128)(2,1)} %get-tuple-element.19.refs_0_, bf16[256,1024]{1,0:T(8,128)(2,1)} %copy-done.12, bf16[256,1024]{1,0:T(8,128)(2,1)} %collective-permute-done.35.refs_2_, bf16[256,1024]{1,0:T(8,128)(2,1)} %collective-permute-done.36.refs_3_), custom_call_target="tpu_custom_call" | custom-call | tf_op jit(solution)/shard_map/pallas_call | solution.py:406
  (157 shorter events, 29.3 us)
Async XLA Ops:
  0.6 83.4 %copy-start = (bf16[512,512]{1,0:T(8,128)(2,1)S(1)}, bf16[512,512]{1,0:T(8,128)(2,1)}, u32[]{:S(2)}) copy-start(bf16[512,512]{1,0:T(8,128)(2,1)} %param.29) | copy-start | bytes 1572868
  1.8 9.7 %copy-start.7 = (bf16[256,512]{1,0:T(8,128)(2,1)}, bf16[256,512]{1,0:T(8,128)(2,1)S(1)}, u32[]{:S(2)}) copy-start(bf16[256,512]{1,0:T(8,128)(2,1)S(1)} %get-tuple-element.29.refs_8_) | copy-start | bytes 786436
  1.8 14.3 %collective-permute-start.6 = (bf16[256,512]{1,0:T(8,128)(2,1)S(1)}, bf16[256,512]{1,0:T(8,128)(2,1)S(1)}, u32[]{:S(2)}, u32[]{:S(2)}) collective-permute-start(bf16[256,512]{1,0:T(8,128)(2,1)S(1)} %get-tuple-element.29.refs_8_), channel_id=1, source_target_pairs={{8,0},{16,8},{24,16},{28,24},{20,28},{12,20},{4,12},{0,4},{9,1},{1... | collective-permute-start | bytes 786440 | tf_op jit(solution)/shard_map/ppermute | solution.py:511
  4.8 13.2 %collective-permute-start = (bf16[256,512]{1,0:T(8,128)(2,1)S(1)}, bf16[256,512]{1,0:T(8,128)(2,1)S(1)}, u32[]{:S(2)}, u32[]{:S(2)}) collective-permute-start(bf16[256,512]{1,0:T(8,128)(2,1)S(1)} %get-tuple-element.30.refs_0_), channel_id=1, source_target_pairs={{0,8},{8,16},{16,24},{24,28},{28,20},{20,12},{12,4},{4,0},{1,9},{9... | collective-permute-start | bytes 786440 | tf_op jit(solution)/shard_map/ppermute | solution.py:510
  7.0 11.2 %copy-start.6 = (bf16[3,512,512]{2,1,0:T(8,128)(2,1)S(1)}, bf16[3,512,512]{2,1,0:T(8,128)(2,1)}, u32[]{:S(2)}) copy-start(bf16[3,512,512]{2,1,0:T(8,128)(2,1)} %param.22) | copy-start | bytes 4718596
  12.8 63.3 %all-to-all-start = ((bf16[4,8,512]{2,1,0:T(8,128)(2,1)}), bf16[4,8,512]{2,1,0:T(8,128)(2,1)S(1)}, u32[]{:S(2)}, u32[]{:S(2)}) async-start(bf16[4,8,512]{2,1,0:T(8,128)(2,1)} %broadcast_in_dim.8), calls=%async_computation | async-start | bytes 65536 | tf_op jit(solution)/shard_map/all_to_all | solution.py:553
  16.1 18.9 %copy-start.16 = (bf16[256,512]{1,0:T(8,128)(2,1)}, bf16[256,512]{1,0:T(8,128)(2,1)S(1)}, u32[]{:S(2)}) copy-start(bf16[256,512]{1,0:T(8,128)(2,1)S(1)} %collective-permute-done.6.refs_15_) | copy-start | bytes 786436
  16.1 8.9 %collective-permute-start.7 = (bf16[256,512]{1,0:T(8,128)(2,1)S(1)}, bf16[256,512]{1,0:T(8,128)(2,1)S(1)}, u32[]{:S(2)}, u32[]{:S(2)}) collective-permute-start(bf16[256,512]{1,0:T(8,128)(2,1)S(1)} %collective-permute-done.6.refs_15_), channel_id=1, source_target_pairs={{8,0},{16,8},{24,16},{28,24},{20,28},{12,20},{4,12},{0,4},{9,1},{1... | collective-permute-start | bytes 786440 | tf_op jit(solution)/shard_map/ppermute | solution.py:511
  18.0 17.0 %copy-start.17 = (bf16[256,512]{1,0:T(8,128)(2,1)}, bf16[256,512]{1,0:T(8,128)(2,1)S(1)}, u32[]{:S(2)}) copy-start(bf16[256,512]{1,0:T(8,128)(2,1)S(1)} %collective-permute-done.refs_1_) | copy-start | bytes 786436
  18.0 8.6 %collective-permute-start.1 = (bf16[256,512]{1,0:T(8,128)(2,1)S(1)}, bf16[256,512]{1,0:T(8,128)(2,1)S(1)}, u32[]{:S(2)}, u32[]{:S(2)}) collective-permute-start(bf16[256,512]{1,0:T(8,128)(2,1)S(1)} %collective-permute-done.refs_1_), channel_id=1, source_target_pairs={{0,8},{8,16},{16,24},{24,28},{28,20},{20,12},{12,4},{4,0},{1,9},{9... | collective-permute-start | bytes 786440 | tf_op jit(solution)/shard_map/ppermute | solution.py:510
  25.0 17.3 %copy-start.18 = (bf16[256,512]{1,0:T(8,128)(2,1)}, bf16[256,512]{1,0:T(8,128)(2,1)S(1)}, u32[]{:S(2)}) copy-start(bf16[256,512]{1,0:T(8,128)(2,1)S(1)} %collective-permute-done.7.refs_14_) | copy-start | bytes 786436
  25.0 8.0 %collective-permute-start.8 = (bf16[256,512]{1,0:T(8,128)(2,1)S(1)}, bf16[256,512]{1,0:T(8,128)(2,1)S(1)}, u32[]{:S(2)}, u32[]{:S(2)}) collective-permute-start(bf16[256,512]{1,0:T(8,128)(2,1)S(1)} %collective-permute-done.7.refs_14_), channel_id=1, source_target_pairs={{8,0},{16,8},{24,16},{28,24},{20,28},{12,20},{4,12},{0,4},{9,1},{1... | collective-permute-start | bytes 786440 | tf_op jit(solution)/shard_map/ppermute | solution.py:511
  26.7 15.6 %copy-start.19 = (bf16[256,512]{1,0:T(8,128)(2,1)}, bf16[256,512]{1,0:T(8,128)(2,1)S(1)}, u32[]{:S(2)}) copy-start(bf16[256,512]{1,0:T(8,128)(2,1)S(1)} %collective-permute-done.1.refs_2_) | copy-start | bytes 786436
  26.7 7.8 %collective-permute-start.2 = (bf16[256,512]{1,0:T(8,128)(2,1)S(1)}, bf16[256,512]{1,0:T(8,128)(2,1)S(1)}, u32[]{:S(2)}, u32[]{:S(2)}) collective-permute-start(bf16[256,512]{1,0:T(8,128)(2,1)S(1)} %collective-permute-done.1.refs_2_), channel_id=1, source_target_pairs={{0,8},{8,16},{16,24},{24,28},{28,20},{20,12},{12,4},{4,0},{1,9},{9... | collective-permute-start | bytes 786440 | tf_op jit(solution)/shard_map/ppermute | solution.py:510
  27.0 15.3 %copy-start.24 = (f32[32,512]{1,0:T(8,128)S(1)}, f32[32,512]{1,0:T(8,128)}, u32[]{:S(2)}) copy-start(f32[32,512]{1,0:T(8,128)} %constant.39.clone) | copy-start | bytes 196612
  27.0 15.3 %copy-start.25 = (f32[8,32]{1,0:T(8,128)S(1)}, f32[8,32]{1,0:T(8,128)}, u32[]{:S(2)}) copy-start(f32[8,32]{1,0:T(8,128)} %param.23) | copy-start | bytes 3076
  33.0 16.3 %copy-start.20 = (bf16[256,512]{1,0:T(8,128)(2,1)}, bf16[256,512]{1,0:T(8,128)(2,1)S(1)}, u32[]{:S(2)}) copy-start(bf16[256,512]{1,0:T(8,128)(2,1)S(1)} %collective-permute-done.8.refs_13_) | copy-start | bytes 786436
  33.0 7.2 %collective-permute-start.9 = (bf16[256,512]{1,0:T(8,128)(2,1)S(1)}, bf16[256,512]{1,0:T(8,128)(2,1)}, u32[]{:S(2)}, u32[]{:S(2)}) collective-permute-start(bf16[256,512]{1,0:T(8,128)(2,1)S(1)} %collective-permute-done.8.refs_13_), channel_id=1, source_target_pairs={{8,0},{16,8},{24,16},{28,24},{20,28},{12,20},{4,12},{0,4},{9,1},{1... | collective-permute-start | bytes 786440 | tf_op jit(solution)/shard_map/ppermute | solution.py:511
  34.4 7.0 %collective-permute-start.3 = (bf16[256,512]{1,0:T(8,128)(2,1)S(1)}, bf16[256,512]{1,0:T(8,128)(2,1)}, u32[]{:S(2)}, u32[]{:S(2)}) collective-permute-start(bf16[256,512]{1,0:T(8,128)(2,1)S(1)} %collective-permute-done.2.refs_3_), channel_id=1, source_target_pairs={{0,8},{8,16},{16,24},{24,28},{28,20},{20,12},{12,4},{4,0},{1,9},{9... | collective-permute-start | bytes 786440 | tf_op jit(solution)/shard_map/ppermute | solution.py:510
  35.1 30.7 %copy-start.27 = (s32[4]{0:T(128)S(1)}, s32[4]{0:T(128)}, u32[]{:S(2)}) copy-start(s32[4]{0:T(128)} %param.19) | copy-start | bytes 52
  40.2 7.1 %collective-permute-start.10 = (bf16[256,512]{1,0:T(8,128)(2,1)}, bf16[256,512]{1,0:T(8,128)(2,1)S(1)}, u32[]{:S(2)}, u32[]{:S(2)}) collective-permute-start(bf16[256,512]{1,0:T(8,128)(2,1)} %collective-permute-done.9.refs_12_), channel_id=1, source_target_pairs={{8,0},{16,8},{24,16},{28,24},{20,28},{12,20},{4,12},{0,4},{9,1},{1... | collective-permute-start | bytes 786440 | tf_op jit(solution)/shard_map/ppermute | solution.py:511
  41.4 7.3 %collective-permute-start.4 = (bf16[256,512]{1,0:T(8,128)(2,1)}, bf16[256,512]{1,0:T(8,128)(2,1)}, u32[]{:S(2)}, u32[]{:S(2)}) collective-permute-start(bf16[256,512]{1,0:T(8,128)(2,1)} %collective-permute-done.3.refs_4_), channel_id=1, source_target_pairs={{0,8},{8,16},{16,24},{24,28},{28,20},{20,12},{12,4},{4,0},{1,9},{9... | collective-permute-start | bytes 786440 | tf_op jit(solution)/shard_map/ppermute | solution.py:510
  47.3 18.5 %copy-start.22 = (bf16[256,512]{1,0:T(8,128)(2,1)}, bf16[256,512]{1,0:T(8,128)(2,1)S(1)}, u32[]{:S(2)}) copy-start(bf16[256,512]{1,0:T(8,128)(2,1)S(1)} %collective-permute-done.10.refs_11_) | copy-start | bytes 786436
  47.3 6.7 %collective-permute-start.11 = (bf16[256,512]{1,0:T(8,128)(2,1)S(1)}, bf16[256,512]{1,0:T(8,128)(2,1)S(1)}, u32[]{:S(2)}, u32[]{:S(2)}) collective-permute-start(bf16[256,512]{1,0:T(8,128)(2,1)S(1)} %collective-permute-done.10.refs_11_), channel_id=1, source_target_pairs={{8,0},{16,8},{24,16},{28,24},{20,28},{12,20},{4,12},{0,4},{9,1},{1... | collective-permute-start | bytes 786440 | tf_op jit(solution)/shard_map/ppermute | solution.py:511
  48.7 7.2 %collective-permute-start.5 = (bf16[256,512]{1,0:T(8,128)(2,1)}, bf16[256,512]{1,0:T(8,128)(2,1)}, u32[]{:S(2)}, u32[]{:S(2)}) collective-permute-start(bf16[256,512]{1,0:T(8,128)(2,1)} %collective-permute-done.4.refs_5_), channel_id=1, source_target_pairs={{0,8},{8,16},{16,24},{24,28},{28,20},{20,12},{12,4},{4,0},{1,9},{9... | collective-permute-start | bytes 786440 | tf_op jit(solution)/shard_map/ppermute | solution.py:510
  54.0 22.1 %copy-start.23 = (bf16[256,512]{1,0:T(8,128)(2,1)}, bf16[256,512]{1,0:T(8,128)(2,1)S(1)}, u32[]{:S(2)}) copy-start(bf16[256,512]{1,0:T(8,128)(2,1)S(1)} %collective-permute-done.11.refs_10_) | copy-start | bytes 786436
  55.9 28.4 %collective-permute-start.19 = (bf16[512,768]{1,0:T(8,128)(2,1)S(1)}, bf16[512,768]{1,0:T(8,128)(2,1)}, u32[]{:S(2)}, u32[]{:S(2)}) collective-permute-start(bf16[512,768]{1,0:T(8,128)(2,1)S(1)} %pad_maximum_fusion.1), channel_id=1, source_target_pairs={{8,0},{16,8},{24,16},{28,24},{20,28},{12,20},{4,12},{0,4},{9,1},{1... | collective-permute-start | bytes 2359304 | tf_op jit(solution)/shard_map/ppermute | solution.py:535
  57.5 33.1 %collective-permute-start.12 = (bf16[512,768]{1,0:T(8,128)(2,1)S(1)}, bf16[512,768]{1,0:T(8,128)(2,1)}, u32[]{:S(2)}, u32[]{:S(2)}) collective-permute-start(bf16[512,768]{1,0:T(8,128)(2,1)S(1)} %pad_maximum_fusion), channel_id=1, source_target_pairs={{0,8},{8,16},{16,24},{24,28},{28,20},{20,12},{12,4},{4,0},{1,9},{9... | collective-permute-start | bytes 2359304 | tf_op jit(solution)/shard_map/ppermute | solution.py:534
  57.9 20.0 %collective-permute-start.29 = (bf16[256,512]{1,0:T(8,128)(2,1)}, bf16[256,512]{1,0:T(8,128)(2,1)}, u32[]{:S(2)}, u32[]{:S(2)}) collective-permute-start(bf16[256,512]{1,0:T(8,128)(2,1)} %collective-permute-done.5.refs_6_), channel_id=1, source_target_pairs={{0,8},{8,16},{16,24},{24,28},{28,20},{20,12},{12,4},{4,0},{1,9},{9... | collective-permute-start | bytes 786440 | tf_op jit(solution)/shard_map/ppermute | solution.py:510
  59.2 18.7 %collective-permute-start.30 = (bf16[256,512]{1,0:T(8,128)(2,1)S(1)}, bf16[256,512]{1,0:T(8,128)(2,1)}, u32[]{:S(2)}, u32[]{:S(2)}) collective-permute-start(bf16[256,512]{1,0:T(8,128)(2,1)S(1)} %collective-permute-done.11.refs_10_), channel_id=1, source_target_pairs={{8,0},{16,8},{24,16},{28,24},{20,28},{12,20},{4,12},{0,4},{9,1},{1... | collective-permute-start | bytes 786440 | tf_op jit(solution)/shard_map/ppermute | solution.py:511
  82.4 87.2 %collective-permute-start.31 = (bf16[512,4096]{1,0:T(8,128)(2,1)}, bf16[512,4096]{1,0:T(8,128)(2,1)}, u32[]{:S(2)}, u32[]{:S(2)}) collective-permute-start(bf16[512,4096]{1,0:T(8,128)(2,1)} %shard_map.180.refs_7_), channel_id=1, source_target_pairs={{0,2},{1,3},{2,0},{3,1},{4,6},{5,7},{6,4},{7,5},{8,10},{9,11},{10,... | collective-permute-start | bytes 12582920 | tf_op jit(solution)/shard_map/ppermute | solution.py:501
  84.3 15.4 %collective-permute-start.20 = (bf16[512,768]{1,0:T(8,128)(2,1)}, bf16[512,768]{1,0:T(8,128)(2,1)S(1)}, u32[]{:S(2)}, u32[]{:S(2)}) collective-permute-start(bf16[512,768]{1,0:T(8,128)(2,1)} %collective-permute-done.19), channel_id=1, source_target_pairs={{8,0},{16,8},{24,16},{28,24},{20,28},{12,20},{4,12},{0,4},{9,1},{1... | collective-permute-start | bytes 2359304 | tf_op jit(solution)/shard_map/ppermute | solution.py:535
  86.7 53.3 %all-to-all-start.1 = ((f32[8,16,512]{2,1,0:T(8,128)}), f32[8,16,512]{2,1,0:T(8,128)S(1)}, u32[]{:S(2)}, u32[]{:S(2)}) async-start(f32[8,16,512]{2,1,0:T(8,128)} %broadcast_in_dim.10), calls=%async_computation.1 | async-start | bytes 524288 | tf_op jit(solution)/shard_map/all_to_all | solution.py:567
  90.6 161.9 %collective-permute-start.33 = (bf16[512,4096]{1,0:T(8,128)(2,1)}, bf16[512,4096]{1,0:T(8,128)(2,1)}, u32[]{:S(2)}, u32[]{:S(2)}) collective-permute-start(bf16[512,4096]{1,0:T(8,128)(2,1)} %shard_map.180.refs_7_), channel_id=1, source_target_pairs={{0,1},{1,0},{2,3},{3,2},{4,5},{5,4},{6,7},{7,6},{8,9},{9,8},{10,11... | collective-permute-start | bytes 12582920 | tf_op jit(solution)/shard_map/ppermute | solution.py:501
  90.6 21.8 %collective-permute-start.13 = (bf16[512,768]{1,0:T(8,128)(2,1)}, bf16[512,768]{1,0:T(8,128)(2,1)S(1)}, u32[]{:S(2)}, u32[]{:S(2)}) collective-permute-start(bf16[512,768]{1,0:T(8,128)(2,1)} %collective-permute-done.12), channel_id=1, source_target_pairs={{0,8},{8,16},{16,24},{24,28},{28,20},{20,12},{12,4},{4,0},{1,9},{9... | collective-permute-start | bytes 2359304 | tf_op jit(solution)/shard_map/ppermute | solution.py:534
  99.7 19.3 %collective-permute-start.21 = (bf16[512,768]{1,0:T(8,128)(2,1)S(1)}, bf16[512,768]{1,0:T(8,128)(2,1)}, u32[]{:S(2)}, u32[]{:S(2)}) collective-permute-start(bf16[512,768]{1,0:T(8,128)(2,1)S(1)} %collective-permute-done.20), channel_id=1, source_target_pairs={{8,0},{16,8},{24,16},{28,24},{20,28},{12,20},{4,12},{0,4},{9,1},{1... | collective-permute-start | bytes 2359304 | tf_op jit(solution)/shard_map/ppermute | solution.py:535
  112.4 19.8 %collective-permute-start.14 = (bf16[512,768]{1,0:T(8,128)(2,1)S(1)}, bf16[512,768]{1,0:T(8,128)(2,1)}, u32[]{:S(2)}, u32[]{:S(2)}) collective-permute-start(bf16[512,768]{1,0:T(8,128)(2,1)S(1)} %collective-permute-done.13), channel_id=1, source_target_pairs={{0,8},{8,16},{16,24},{24,28},{28,20},{20,12},{12,4},{4,0},{1,9},{9... | collective-permute-start | bytes 2359304 | tf_op jit(solution)/shard_map/ppermute | solution.py:534
  121.1 19.6 %collective-permute-start.22 = (bf16[512,768]{1,0:T(8,128)(2,1)}, bf16[512,768]{1,0:T(8,128)(2,1)}, u32[]{:S(2)}, u32[]{:S(2)}) collective-permute-start(bf16[512,768]{1,0:T(8,128)(2,1)} %collective-permute-done.21), channel_id=1, source_target_pairs={{8,0},{16,8},{24,16},{28,24},{20,28},{12,20},{4,12},{0,4},{9,1},{1... | collective-permute-start | bytes 2359304 | tf_op jit(solution)/shard_map/ppermute | solution.py:535
  132.2 18.7 %collective-permute-start.15 = (bf16[512,768]{1,0:T(8,128)(2,1)}, bf16[512,768]{1,0:T(8,128)(2,1)S(1)}, u32[]{:S(2)}, u32[]{:S(2)}) collective-permute-start(bf16[512,768]{1,0:T(8,128)(2,1)} %collective-permute-done.14), channel_id=1, source_target_pairs={{0,8},{8,16},{16,24},{24,28},{28,20},{20,12},{12,4},{4,0},{1,9},{9... | collective-permute-start | bytes 2359304 | tf_op jit(solution)/shard_map/ppermute | solution.py:534
  150.9 34.2 %collective-permute-start.23 = (bf16[512,768]{1,0:T(8,128)(2,1)}, bf16[512,768]{1,0:T(8,128)(2,1)S(1)}, u32[]{:S(2)}, u32[]{:S(2)}) collective-permute-start(bf16[512,768]{1,0:T(8,128)(2,1)} %collective-permute-done.22), channel_id=1, source_target_pairs={{8,0},{16,8},{24,16},{28,24},{20,28},{12,20},{4,12},{0,4},{9,1},{1... | collective-permute-start | bytes 2359304 | tf_op jit(solution)/shard_map/ppermute | solution.py:535
  152.2 38.0 %collective-permute-start.16 = (bf16[512,768]{1,0:T(8,128)(2,1)S(1)}, bf16[512,768]{1,0:T(8,128)(2,1)S(1)}, u32[]{:S(2)}, u32[]{:S(2)}) collective-permute-start(bf16[512,768]{1,0:T(8,128)(2,1)S(1)} %collective-permute-done.15), channel_id=1, source_target_pairs={{0,8},{8,16},{16,24},{24,28},{28,20},{20,12},{12,4},{4,0},{1,9},{9... | collective-permute-start | bytes 2359304 | tf_op jit(solution)/shard_map/ppermute | solution.py:534
  152.9 21.8 %copy-start.3 = (f32[1024,768]{1,0:T(8,128)S(1)}, f32[1024,768]{1,0:T(8,128)}, u32[]{:S(2)}) copy-start(f32[1024,768]{1,0:T(8,128)} %convolution_add_fusion.9) | copy-start | bytes 9437188
  169.6 95.0 %collective-permute-start.32 = (bf16[512,4096]{1,0:T(8,128)(2,1)}, bf16[512,4096]{1,0:T(8,128)(2,1)}, u32[]{:S(2)}, u32[]{:S(2)}) collective-permute-start(bf16[512,4096]{1,0:T(8,128)(2,1)} %collective-permute-done.31.refs_4_), channel_id=1, source_target_pairs={{0,1},{1,0},{2,3},{3,2},{4,5},{5,4},{6,7},{7,6},{8,9},{9,8},{10,11... | collective-permute-start | bytes 12582920 | tf_op jit(solution)/shard_map/ppermute | solution.py:501
  180.6 98.3 %all-to-all-start.2 = ((bf16[32,16,512]{2,1,0:T(8,128)(2,1)}), bf16[32,16,512]{2,1,0:T(8,128)(2,1)S(1)}, u32[]{:S(2)}, u32[]{:S(2)}) async-start(bf16[32,16,512]{2,1,0:T(8,128)(2,1)} %bitcast.20), calls=%async_computation.2 | async-start | bytes 1048576 | tf_op jit(solution)/shard_map/all_to_all | solution.py:585
  185.0 28.1 %collective-permute-start.24 = (bf16[512,768]{1,0:T(8,128)(2,1)S(1)}, bf16[512,768]{1,0:T(8,128)(2,1)S(1)}, u32[]{:S(2)}, u32[]{:S(2)}) collective-permute-start(bf16[512,768]{1,0:T(8,128)(2,1)S(1)} %collective-permute-done.23), channel_id=1, source_target_pairs={{8,0},{16,8},{24,16},{28,24},{20,28},{12,20},{4,12},{0,4},{9,1},{1... | collective-permute-start | bytes 2359304 | tf_op jit(solution)/shard_map/ppermute | solution.py:535
  186.9 26.3 %slice-start.2 = ((s8[8388608]{0:T(1024)(128)(4,1)}), s8[4194304]{0:T(1024)(128)(4,1)S(1)}, s32[]{:S(2)}) async-start(s8[8388608]{0:T(1024)(128)(4,1)} %bitcast.57), calls=%async_computation.8 | async-start | bytes 8388608
  190.2 22.9 %slice-start.3 = ((s8[8388608]{0:T(1024)(128)(4,1)}), s8[4194304]{0:T(1024)(128)(4,1)S(1)}, s32[]{:S(2)}) async-start(s8[8388608]{0:T(1024)(128)(4,1)} %bitcast.57), calls=%async_computation.9 | async-start | bytes 8388608
  190.2 23.9 %collective-permute-start.17 = (bf16[512,768]{1,0:T(8,128)(2,1)S(1)}, bf16[512,768]{1,0:T(8,128)(2,1)S(1)}, u32[]{:S(2)}, u32[]{:S(2)}) collective-permute-start(bf16[512,768]{1,0:T(8,128)(2,1)S(1)} %collective-permute-done.16), channel_id=1, source_target_pairs={{0,8},{8,16},{16,24},{24,28},{28,20},{20,12},{12,4},{4,0},{1,9},{9... | collective-permute-start | bytes 2359304 | tf_op jit(solution)/shard_map/ppermute | solution.py:534
  213.1 21.5 %collective-permute-start.25 = (bf16[512,768]{1,0:T(8,128)(2,1)S(1)}, bf16[512,768]{1,0:T(8,128)(2,1)S(1)}, u32[]{:S(2)}, u32[]{:S(2)}) collective-permute-start(bf16[512,768]{1,0:T(8,128)(2,1)S(1)} %collective-permute-done.24), channel_id=1, source_target_pairs={{8,0},{16,8},{24,16},{28,24},{20,28},{12,20},{4,12},{0,4},{9,1},{1... | collective-permute-start | bytes 2359304 | tf_op jit(solution)/shard_map/ppermute | solution.py:535
  214.2 22.6 %collective-permute-start.18 = (bf16[512,768]{1,0:T(8,128)(2,1)S(1)}, bf16[512,768]{1,0:T(8,128)(2,1)S(1)}, u32[]{:S(2)}, u32[]{:S(2)}) collective-permute-start(bf16[512,768]{1,0:T(8,128)(2,1)S(1)} %collective-permute-done.17), channel_id=1, source_target_pairs={{0,8},{8,16},{16,24},{24,28},{28,20},{20,12},{12,4},{4,0},{1,9},{9... | collective-permute-start | bytes 2359304 | tf_op jit(solution)/shard_map/ppermute | solution.py:534
  244.7 7.7 %collective-permute-start.28 = (bf16[256,512]{1,0:T(8,128)(2,1)}, bf16[256,512]{1,0:T(8,128)(2,1)S(1)}, u32[]{:S(2)}, u32[]{:S(2)}) collective-permute-start(bf16[256,512]{1,0:T(8,128)(2,1)} %get-tuple-element.17), channel_id=1, source_target_pairs={{0,1},{1,0},{2,3},{3,2},{4,5},{5,4},{6,7},{7,6},{8,9},{9,8},{10,11... | collective-permute-start | bytes 786440 | tf_op jit(solution)/shard_map/ppermute | solution.py:501
  250.6 9.4 %collective-permute-start.26 = (bf16[256,512]{1,0:T(8,128)(2,1)}, bf16[256,512]{1,0:T(8,128)(2,1)S(1)}, u32[]{:S(2)}, u32[]{:S(2)}) collective-permute-start(bf16[256,512]{1,0:T(8,128)(2,1)} %get-tuple-element.15), channel_id=1, source_target_pairs={{0,2},{1,3},{2,0},{3,1},{4,6},{5,7},{6,4},{7,5},{8,10},{9,11},{10,... | collective-permute-start | bytes 786440 | tf_op jit(solution)/shard_map/ppermute | solution.py:501
  252.0 12.6 %collective-permute-start.27 = (bf16[256,512]{1,0:T(8,128)(2,1)}, bf16[256,512]{1,0:T(8,128)(2,1)S(1)}, u32[]{:S(2)}, u32[]{:S(2)}) collective-permute-start(bf16[256,512]{1,0:T(8,128)(2,1)} %get-tuple-element.16), channel_id=1, source_target_pairs={{0,3},{1,2},{2,1},{3,0},{4,7},{5,6},{6,5},{7,4},{8,11},{9,10},{10,... | collective-permute-start | bytes 786440 | tf_op jit(solution)/shard_map/ppermute | solution.py:501
  252.4 12.2 %copy-start.13 = (bf16[256,512]{1,0:T(8,128)(2,1)}, bf16[256,512]{1,0:T(8,128)(2,1)S(1)}, u32[]{:S(2)}) copy-start(bf16[256,512]{1,0:T(8,128)(2,1)S(1)} %collective-permute-done.28.refs_2_) | copy-start | bytes 786436
  279.0 11.3 %copy-start.11 = (bf16[256,1024]{1,0:T(8,128)(2,1)S(1)}, bf16[256,1024]{1,0:T(8,128)(2,1)}, u32[]{:S(2)}) copy-start(bf16[256,1024]{1,0:T(8,128)(2,1)} %get-tuple-element.20.refs_1_) | copy-start | bytes 1572868
  279.0 11.6 %copy-start.10 = (bf16[256,1024]{1,0:T(8,128)(2,1)S(1)}, bf16[256,1024]{1,0:T(8,128)(2,1)}, u32[]{:S(2)}) copy-start(bf16[256,1024]{1,0:T(8,128)(2,1)} %get-tuple-element.21.refs_2_) | copy-start | bytes 1572868
  279.0 13.2 %copy-start.9 = (bf16[256,1024]{1,0:T(8,128)(2,1)S(1)}, bf16[256,1024]{1,0:T(8,128)(2,1)}, u32[]{:S(2)}) copy-start(bf16[256,1024]{1,0:T(8,128)(2,1)} %get-tuple-element.22.refs_3_) | copy-start | bytes 1572868
  285.9 22.3 %all-to-all-start.3 = ((bf16[32,16,640]{2,1,0:T(8,128)(2,1)}), bf16[32,16,640]{2,1,0:T(8,128)(2,1)S(1)}, u32[]{:S(2)}, u32[]{:S(2)}) async-start(bf16[32,16,640]{2,1,0:T(8,128)(2,1)} %shard_map.184), calls=%async_computation.3 | async-start | bytes 1310720 | tf_op jit(solution)/shard_map/all_to_all | solution.py:602
  290.3 36.8 %collective-permute-start.34 = (bf16[256,1024]{1,0:T(8,128)(2,1)S(1)}, bf16[256,1024]{1,0:T(8,128)(2,1)S(1)}, u32[]{:S(2)}, u32[]{:S(2)}) collective-permute-start(bf16[256,1024]{1,0:T(8,128)(2,1)S(1)} %copy-done.11), channel_id=1, source_target_pairs={{0,1},{1,0},{2,3},{3,2},{4,5},{5,4},{6,7},{7,6},{8,9},{9,8},{10,11... | collective-permute-start | bytes 1572872 | tf_op jit(solution)/shard_map/ppermute | solution.py:501
  290.6 36.5 %collective-permute-start.35 = (bf16[256,1024]{1,0:T(8,128)(2,1)S(1)}, bf16[256,1024]{1,0:T(8,128)(2,1)}, u32[]{:S(2)}, u32[]{:S(2)}) collective-permute-start(bf16[256,1024]{1,0:T(8,128)(2,1)S(1)} %copy-done.10), channel_id=1, source_target_pairs={{0,2},{1,3},{2,0},{3,1},{4,6},{5,7},{6,4},{7,5},{8,10},{9,11},{10,... | collective-permute-start | bytes 1572872 | tf_op jit(solution)/shard_map/ppermute | solution.py:501
  292.2 34.8 %collective-permute-start.36 = (bf16[256,1024]{1,0:T(8,128)(2,1)S(1)}, bf16[256,1024]{1,0:T(8,128)(2,1)}, u32[]{:S(2)}, u32[]{:S(2)}) collective-permute-start(bf16[256,1024]{1,0:T(8,128)(2,1)S(1)} %copy-done.9), channel_id=1, source_target_pairs={{0,3},{1,2},{2,1},{3,0},{4,7},{5,6},{6,5},{7,4},{8,11},{9,10},{10,... | collective-permute-start | bytes 1572872 | tf_op jit(solution)/shard_map/ppermute | solution.py:501
  309.1 22.7 %copy-start.1 = (bf16[512,512]{1,0:T(8,128)(2,1)S(1)}, bf16[512,512]{1,0:T(8,128)(2,1)}, u32[]{:S(2)}) copy-start(bf16[512,512]{1,0:T(8,128)(2,1)} %param.29) | copy-start | bytes 1572868
  311.8 10.8 %all-to-all-start.4 = ((f32[8,8,512]{2,1,0:T(8,128)}), f32[8,8,512]{2,1,0:T(8,128)S(1)}, u32[]{:S(2)}, u32[]{:S(2)}) async-start(f32[8,8,512]{2,1,0:T(8,128)} %shard_map.185), calls=%async_computation.4 | async-start | bytes 262144 | tf_op jit(solution)/shard_map/all_to_all | solution.py:607
  323.8 7.4 %all-to-all-start.5 = ((f32[4,8,128]{2,1,0:T(8,128)}), f32[4,8,128]{2,1,0:T(8,128)S(1)}, u32[]{:S(2)}, u32[]{:S(2)}) async-start(f32[4,8,128]{2,1,0:T(8,128)} %convolution_bitcast_fusion.1), calls=%async_computation.5 | async-start | bytes 32768 | tf_op jit(solution)/shard_map/all_to_all | solution.py:610
  (11 other events, 50.9 us)
where the time goes:
time: 333 us; the launch traced here: 332 us
  waiting for transfers between devices  153 us (46%)
  Pallas kernels  61.2 us (18%)
  starting transfers between devices  59.1 us (18%)
  matrix products  39.9 us (12%)
  local copies, waits for them, and re-layouts  14.6 us (4%)
    ppermute x7, waiting for transfers between devices, program(): second_block = lax.ppermute(second_block, 'psg', ring.backward)  42.6 us
    dot_general x16, matrix products, term(): return jnp.dot(part, block, preferred_element_type=F32)  37.6 us
    ppermute x7, waiting for transfers between devices, program(): first_block = lax.ppermute(first_block, 'psg', ring.forward)  32.5 us
    ppermute x9, waiting for transfers between devices, swap(): return lax.ppermute(value, 'mp', [(i, i ^ k) for i in range(groups)])  28.9 us
    ppermute x7, waiting for transfers between devices, program(): down.append(lax.ppermute(down[-1], 'psg', ring.backward))  24.3 us
    all_to_all x1, waiting for transfers between devices, program(): got = lax.all_to_all(pooled, ('psg', 'mp'), 0, 0, tiled=True)  15.2 us
    pallas_call x1, Pallas kernels, project(): pl.pallas_call(project_kernel, out_shape=[jax.ShapeDtypeStruct((rows, sha...  13.6 us
    pallas_call x2, Pallas kernels, attend(): pl.pallas_call(functools.partial(attend_kernel, away=tuple(away)), out_sh...  11.6 us
  transfers between devices with their start and end apart: 43, of which 20 were waited for; matrix products, arithmetic and copies ran while one was open for 16% of the time, Pallas kernels for 17%

commit v1 on v0

--- a/solution.py
+++ b/solution.py
@@ -25,6 +25,7 @@
 F32 = jnp.float32
 BF16 = jnp.bfloat16
 LANES = 128
+MIB = 1 << 20
 
 
 def bucket_onehot(length, buckets, max_distance):
@@ -101,6 +102,7 @@
     spec = pl.BlockSpec((SEQ, model), lambda i, t: (i, 0))
     return pl.pallas_call(
         norm_kernel,
+        compiler_params=pltpu.CompilerParams(vmem_limit_bytes=24 * MIB),
         out_shape=jax.ShapeDtypeStruct((rows, model), BF16),
         grid_spec=pltpu.PrefetchScalarGridSpec(
             num_scalar_prefetch=1,
@@ -126,6 +128,7 @@
     length = width // 2
     return pl.pallas_call(
         bias_kernel,
+        compiler_params=pltpu.CompilerParams(vmem_limit_bytes=8 * MIB),
         out_shape=jax.ShapeDtypeStruct((heads, length, length), F32),
         grid=(heads,),
         in_specs=[pl.BlockSpec((1, 1, width), lambda h: (h, 0, 0))],
@@ -160,6 +163,7 @@
 
     return pl.pallas_call(
         lookup_kernel,
+        compiler_params=pltpu.CompilerParams(vmem_limit_bytes=8 * MIB),
         out_shape=jax.ShapeDtypeStruct((count, width), F32),
         grid_spec=pltpu.PrefetchScalarGridSpec(
             num_scalar_prefetch=2,
@@ -216,6 +220,7 @@
         specs += [pl.BlockSpec((SEQ, first.shape[1]), lambda i, n, g, k=k: (g[0] ^ k, 0))] * 2
     return pl.pallas_call(
         functools.partial(attend_kernel, away=tuple(away)),
+        compiler_params=pltpu.CompilerParams(vmem_limit_bytes=24 * MIB),
         out_shape=[jax.ShapeDtypeStruct((SEQ, 2 * width), BF16)] * count,
         grid_spec=pltpu.PrefetchScalarGridSpec(
             num_scalar_prefetch=2,
@@ -246,6 +251,7 @@
     shape = (2 * cut, width * len(uppers))
     return pl.pallas_call(
         join_kernel,
+        compiler_params=pltpu.CompilerParams(vmem_limit_bytes=16 * MIB),
         out_shape=jax.ShapeDtypeStruct(shape, uppers[0].dtype),
         in_specs=[vmem] * (2 * len(uppers)),
         out_specs=vmem,
@@ -287,6 +293,7 @@
 
     return pl.pallas_call(
         project_kernel,
+        compiler_params=pltpu.CompilerParams(vmem_limit_bytes=58 * MIB),
         out_shape=[jax.ShapeDtypeStruct((rows, share), BF16)] * groups,
         grid_spec=pltpu.PrefetchScalarGridSpec(
             num_scalar_prefetch=2,
@@ -380,6 +387,7 @@
     vmem = pl.BlockSpec(memory_space=pltpu.VMEM)
     return pl.pallas_call(
         cross_kernel,
+        compiler_params=pltpu.CompilerParams(vmem_limit_bytes=24 * MIB),
         out_shape=jax.ShapeDtypeStruct((devices, heads, width + LANES), BF16),
         in_specs=[smem, smem, smem] + [vmem] * (2 + groups),
         out_specs=vmem,
@@ -405,6 +413,7 @@
     rows, width = blocks[0].shape
     return pl.pallas_call(
         gather_kernel,
+        compiler_params=pltpu.CompilerParams(vmem_limit_bytes=8 * MIB),
         out_shape=jax.ShapeDtypeStruct((len(blocks) * rows, width), blocks[0].dtype),
         grid_spec=pltpu.PrefetchScalarGridSpec(
             num_scalar_prefetch=1,
@@ -451,7 +460,7 @@
     head = lax.broadcasted_iota(jnp.int32, value.shape, 1) // HEAD_DIM
     own = head == lax.rem(lax.broadcasted_iota(jnp.int32, value.shape, 0), heads)
     value = jnp.where(own, value, 0.0).reshape(CLAIMS * POS, heads, weight.shape[1])
-    value = jnp.sum(value, axis=1)
+    value = jnp.sum(value, axis=1).astype(BF16)
     for copy in range(out_ref.shape[0]):
         out_ref[copy] = value
 
@@ -460,10 +469,37 @@
     vmem = pl.BlockSpec(memory_space=pltpu.VMEM)
     return pl.pallas_call(
         combine_kernel,
-        out_shape=jax.ShapeDtypeStruct((copies, CLAIMS * POS, weight.shape[1]), F32),
+        compiler_params=pltpu.CompilerParams(vmem_limit_bytes=16 * MIB),
+        out_shape=jax.ShapeDtypeStruct((copies, CLAIMS * POS, weight.shape[1]), BF16),
         in_specs=[vmem, vmem, vmem],
         out_specs=vmem,
     )(owner, got, weight)
+
+
+def finish_kernel(group_ref, got_ref, residual_ref, *refs):
+    weight_refs, out_ref = refs[:-1], refs[-1]
+    groups = len(weight_refs)
+    total = residual_ref[...]
+    for k, weight_ref in enumerate(weight_refs):
+        source = group_ref[0] ^ k
+        value = jnp.zeros(got_ref.shape[1:], F32)
+        for block in range(got_ref.shape[0] // groups):
+            value = value + got_ref[block * groups + source].astype(F32)
+        for part in split2(value):
+            total = total + jnp.dot(part, weight_ref[...], preferred_element_type=F32)
+    out_ref[...] = total.astype(BF16)
+
+
+def finish(group, got, residual, weights):
+    smem = pl.BlockSpec(memory_space=pltpu.SMEM)
+    vmem = pl.BlockSpec(memory_space=pltpu.VMEM)
+    return pl.pallas_call(
+        finish_kernel,
+        compiler_params=pltpu.CompilerParams(vmem_limit_bytes=8 * MIB),
+        out_shape=jax.ShapeDtypeStruct(residual.shape, BF16),
+        in_specs=[smem] + [vmem] * (2 + len(weights)),
+        out_specs=vmem,
+    )(group, got, residual, *weights)
 
 
 def program(
@@ -529,7 +565,7 @@
 
     own_blocks = (first_block, second_block)
     arrived = [own_blocks]
-    late = (psg - 1) // 2
+    late = psg - 3
     for step in range(1, psg):
         first_block = lax.ppermute(first_block, "psg", ring.forward)
         second_block = lax.ppermute(second_block, "psg", ring.backward)
@@ -554,6 +590,11 @@
         jnp.broadcast_to(found[None], (groups,) + found.shape), "mp", 0, 0, tiled=True
     )
     embedded = jnp.sum(found_all.astype(F32), axis=0)
+    residual = lax.dynamic_slice_in_dim(embedded, group * piece, piece, 1)
+    final_weights = []
+    for k in range(groups):
+        block = lax.dynamic_slice_in_dim(cross_output, (group ^ k) * piece, piece, 1)
+        final_weights.append(swap(block, k) if k else block)
     query_part = jnp.dot(
         embedded * dec_gain, cross_query.astype(F32), precision=HIGHEST
     )
@@ -567,7 +608,7 @@
     messages = lax.all_to_all(
         jnp.broadcast_to(message[None], (psg,) + message.shape), "psg", 0, 0, tiled=True
     )
-    messages = after(messages, arrived[min(4, psg - 1)])
+    messages = after(messages, arrived[min(5, psg - 1)])
     joined = jnp.sum(messages[:, : query_rows + 1], axis=0)
     inverse_dec = lax.rsqrt(joined[query_rows, :query_rows] / D + EPSILON)
     cquery = (joined[:query_rows] * inverse_dec[:, None]).reshape(
@@ -603,15 +644,9 @@
     blocks = [swap(rows[k], k) if k else rows[0] for k in range(groups)]
     encoded = in_passage_order(here_1, blocks)
     owner_row = jnp.repeat(owners, POS * heads_here).reshape(1, -1)
-    value_part = combine(owner_row, got, cross_keyval[1], psg)
-    values = lax.all_to_all(value_part, "psg", 0, 0, tiled=True)
-    cross_attn = jnp.sum(values, axis=0)
-    out_part = jnp.dot(cross_attn, cross_output.astype(F32), precision=HIGHEST)
-    out_parts = lax.all_to_all(
-        out_part.reshape(query_rows, groups, piece).transpose(1, 0, 2), "mp", 0, 0, tiled=True
-    )
-    residual = lax.dynamic_slice_in_dim(embedded, group * piece, piece, 1)
-    decoded = (residual + jnp.sum(out_parts, axis=0)).astype(BF16).reshape(CLAIMS, POS, piece)
+    value_part = combine(owner_row, got, cross_keyval[1], psg * groups)
+    values = lax.all_to_all(value_part, ("psg", "mp"), 0, 0, tiled=True)
+    decoded = finish(here_1, values, residual, final_weights).reshape(CLAIMS, POS, piece)
     return (encoded, decoded)
 
 

time: 333 us -> 329 us (0.988)
  local copies, waits for them, and re-layouts: 14.6 us -> 38.1 us
  Pallas kernels: 61.2 us -> 40.2 us
    unnamed x66 -> x110, local copies, waits for them, and re-layouts: 4.96 us -> 26.9 us
    pallas_call x10 -> x11, Pallas kernels: 61.2 us -> 40.2 us  [the longest x1 13.8 us: project(): pl.pallas_call(project_kernel, compiler_params=pltpu.CompilerParams(vmem_...]
    ppermute x7, waiting for transfers between devices: 32.5 us -> 46.9 us  [program(): first_block = lax.ppermute(first_block, 'psg', ring.forward)]
    ppermute x7, waiting for transfers between devices: 42.6 us -> 30.2 us  [program(): second_block = lax.ppermute(second_block, 'psg', ring.backward)]
    all_to_all x2 -> x1, waiting for transfers between devices: 6.13 us -> 0.01 us  [program(): values = lax.all_to_all(value_part, ('psg', 'mp'), 0, 0, tiled=True)]
    ppermute x9 -> x12, waiting for transfers between devices: 28.9 us -> 33.3 us  [swap(): return lax.ppermute(value, 'mp', [(i, i ^ k) for i in range(groups)])]
    ppermute x7, waiting for transfers between devices: 24.3 us -> 20.7 us  [program(): down.append(lax.ppermute(down[-1], 'psg', ring.backward))]
    ppermute x9 -> x12, starting transfers between devices: 5.23 us -> 7.19 us  [swap(): return lax.ppermute(value, 'mp', [(i, i ^ k) for i in range(groups)])]
  transfers between devices with their start and end apart: 43 -> 45, of which waited for: 20 -> 25; matrix products, arithmetic and copies ran while one was open for 16% -> 16% of each run, Pallas kernels for 17% -> 11%
where the time goes in v1:
time: 329 us; the launch traced here: 327 us
  waiting for transfers between devices  152 us (46%)
  starting transfers between devices  55.8 us (17%)
  Pallas kernels  40.2 us (12%)
  local copies, waits for them, and re-layouts  38.1 us (12%)
  matrix products  36.8 us (11%)
    ppermute x7, waiting for transfers between devices, program(): first_block = lax.ppermute(first_block, 'psg', ring.forward)  46.9 us
    dot_general x16, matrix products, term(): return jnp.dot(part, block, preferred_element_type=F32)  35.7 us
    ppermute x12, waiting for transfers between devices, swap(): return lax.ppermute(value, 'mp', [(i, i ^ k) for i in range(groups)])  33.3 us
    ppermute x7, waiting for transfers between devices, program(): second_block = lax.ppermute(second_block, 'psg', ring.backward)  30.2 us
    unnamed x110, local copies, waits for them, and re-layouts  26.9 us
    ppermute x7, waiting for transfers between devices, program(): down.append(lax.ppermute(down[-1], 'psg', ring.backward))  20.7 us
    all_to_all x1, waiting for transfers between devices, program(): got = lax.all_to_all(pooled, ('psg', 'mp'), 0, 0, tiled=True)  15.8 us
    pallas_call x1, Pallas kernels, project(): pl.pallas_call(project_kernel, compiler_params=pltpu.CompilerParams(vmem_...  13.8 us
  transfers between devices with their start and end apart: 45, of which 25 were waited for; matrix products, arithmetic and copies ran while one was open for 16% of the time, Pallas kernels for 11%

profile of v1, /device:TPU:0, one launch (start us, length us, event | category | flops | bytes accessed | tf_op | source)
XLA Modules:
  0.0 327.1 jit_solution(2089650301605191317)
XLA Ops:
  1.8 3.0 collective-permute-start.6
  5.9 3.3 %copy-done.4 = bf16[8032,512]{1,0:T(8,128)(2,1)S(1)} copy-done((bf16[8032,512]{1,0:T(8,128)(2,1)S(1)}, bf16[8032,512]{1,0:T(8,128)(2,1)}, u32[]{:S(2)}) %copy-start.4) | copy-done | bytes 8224792
  10.7 3.3 all-to-all-start
  13.9 1.9 collective-permute-start.7
  16.0 1.5 slice_bitcast_fusion.3
  17.5 5.3 %collective-permute-done.7.refs_14_ = bf16[256,512]{1,0:T(8,128)(2,1)S(1)} collective-permute-done((bf16[256,512]{1,0:T(8,128)(2,1)S(1)}, bf16[256,512]{1,0:T(8,128)(2,1)S(1)}, u32[]{:S(2)}, u32[]{:S(2)}) %collective-permute-start.7) | collective-permute-done | bytes 262176 | tf_op jit(solution)/shard_map/ppermute | solution.py:547
  22.8 1.7 collective-permute-start.8
  24.9 5.9 %collective-permute-done.8.refs_13_ = bf16[256,512]{1,0:T(8,128)(2,1)S(1)} collective-permute-done((bf16[256,512]{1,0:T(8,128)(2,1)S(1)}, bf16[256,512]{1,0:T(8,128)(2,1)S(1)}, u32[]{:S(2)}, u32[]{:S(2)}) %collective-permute-start.8) | collective-permute-done | bytes 262176 | tf_op jit(solution)/shard_map/ppermute | solution.py:547
  30.8 1.4 collective-permute-start.9
  33.9 4.1 %collective-permute-done.9.refs_12_ = bf16[256,512]{1,0:T(8,128)(2,1)S(1)} collective-permute-done((bf16[256,512]{1,0:T(8,128)(2,1)S(1)}, bf16[256,512]{1,0:T(8,128)(2,1)S(1)}, u32[]{:S(2)}, u32[]{:S(2)}) %collective-permute-start.9) | collective-permute-done | bytes 262176 | tf_op jit(solution)/shard_map/ppermute | solution.py:547
  41.1 3.7 %collective-permute-done.10.refs_11_ = bf16[256,512]{1,0:T(8,128)(2,1)S(1)} collective-permute-done((bf16[256,512]{1,0:T(8,128)(2,1)S(1)}, bf16[256,512]{1,0:T(8,128)(2,1)S(1)}, u32[]{:S(2)}, u32[]{:S(2)}) %collective-permute-start.10) | collective-permute-done | bytes 262176 | tf_op jit(solution)/shard_map/ppermute | solution.py:547
  44.8 1.4 collective-permute-start.11
  47.5 2.2 slice_bitcast_fusion
  49.8 1.6 collective-permute-done.11.refs_10_
  51.4 1.4 collective-permute-done.5.refs_6_
  52.7 1.6 collective-permute-start.19
  54.8 1.8 collective-permute-start.29
  58.6 2.0 copy.31
  60.6 3.4 %copy-done.3 = bf16[1024,4096]{1,0:T(8,128)(2,1)S(1)} copy-done((bf16[1024,4096]{1,0:T(8,128)(2,1)S(1)}, bf16[1024,4096]{1,0:T(8,128)(2,1)}, u32[]{:S(2)}) %copy-start.3) | copy-done | bytes 8388632
  64.0 4.4 %shard_map.177 = bf16[1024,4096]{1,0:T(8,128)(2,1)S(1)} custom-call(s32[8]{0:T(128)S(1)} %get-tuple-element.41.table_ref, bf16[1024,4096]{1,0:T(8,128)(2,1)S(1)} %copy-done.3, f32[1,4096]{1,0:T(1,128)S(1)} %bitcast.50), custom_call_target="tpu_custom_call" | custom-call | flops 25165824 | bytes 16777216 | tf_op jit(solution)/shard_map/pallas_call | solution.py:103
  68.4 3.3 %copy-done.2 = bf16[1024,4096]{1,0:T(8,128)(2,1)} copy-done((bf16[1024,4096]{1,0:T(8,128)(2,1)}, bf16[1024,4096]{1,0:T(8,128)(2,1)S(1)}, u32[]{:S(2)}) %copy-start.2) | copy-done | bytes 8388632
  71.8 3.5 %collective-permute-done.29.refs_7_ = bf16[256,512]{1,0:T(8,128)(2,1)} collective-permute-done((bf16[256,512]{1,0:T(8,128)(2,1)}, bf16[256,512]{1,0:T(8,128)(2,1)}, u32[]{:S(2)}, u32[]{:S(2)}) %collective-permute-start.29) | collective-permute-done | bytes 262176 | tf_op jit(solution)/shard_map/ppermute | solution.py:546
  83.8 3.6 %shard_map.180.refs_7_ = bf16[512,4096]{1,0:T(8,128)(2,1)} custom-call(bf16[256,512]{1,0:T(8,128)(2,1)S(1)} %get-tuple-element.34.refs_0_, bf16[256,512]{1,0:T(8,128)(2,1)S(1)} %copy-done.15, bf16[256,512]{1,0:T(8,128)(2,1)S(1)} %copy-done.19, bf16[256,512]{1,0:T(8,128)(2,1)S(1)} %copy-done.23, bf16[256,512]{1,0:T(8,128)(2,1)S(1)} %copy-done.27, ...), custom_call_target="tpu_custom_call" | custom-call | bytes 8388608 | tf_op jit(solution)/shard_map/pallas_call | solution.py:252
  89.2 1.6 collective-permute-start.20
  91.5 4.1 %all-to-all-start.1 = ((f32[8,16,512]{2,1,0:T(8,128)}), f32[8,16,512]{2,1,0:T(8,128)S(1)}, u32[]{:S(2)}, u32[]{:S(2)}) async-start(f32[8,16,512]{2,1,0:T(8,128)} %broadcast_in_dim.10), calls=%async_computation.1 | async-start | bytes 524288 | tf_op jit(solution)/shard_map/all_to_all | solution.py:608
  95.7 2.1 collective-permute-start.13
  97.7 2.6 fusion.1
  100.3 2.6 fusion.17
  102.9 1.9 collective-permute-done.20
  106.1 11.4 %collective-permute-done.13 = bf16[512,768]{1,0:T(8,128)(2,1)S(1)} collective-permute-done((bf16[512,768]{1,0:T(8,128)(2,1)}, bf16[512,768]{1,0:T(8,128)(2,1)S(1)}, u32[]{:S(2)}, u32[]{:S(2)}) %collective-permute-start.13) | collective-permute-done | bytes 786464 | tf_op jit(solution)/shard_map/ppermute | solution.py:570
  119.4 4.6 %collective-permute-done.21 = bf16[512,768]{1,0:T(8,128)(2,1)S(1)} collective-permute-done((bf16[512,768]{1,0:T(8,128)(2,1)S(1)}, bf16[512,768]{1,0:T(8,128)(2,1)S(1)}, u32[]{:S(2)}, u32[]{:S(2)}) %collective-permute-start.21) | collective-permute-done | bytes 786464 | tf_op jit(solution)/shard_map/ppermute | solution.py:571
  125.0 12.2 %collective-permute-done.14 = bf16[512,768]{1,0:T(8,128)(2,1)S(1)} collective-permute-done((bf16[512,768]{1,0:T(8,128)(2,1)S(1)}, bf16[512,768]{1,0:T(8,128)(2,1)S(1)}, u32[]{:S(2)}, u32[]{:S(2)}) %collective-permute-start.14) | collective-permute-done | bytes 786464 | tf_op jit(solution)/shard_map/ppermute | solution.py:570
  138.5 4.9 %collective-permute-done.22 = bf16[512,768]{1,0:T(8,128)(2,1)S(1)} collective-permute-done((bf16[512,768]{1,0:T(8,128)(2,1)S(1)}, bf16[512,768]{1,0:T(8,128)(2,1)S(1)}, u32[]{:S(2)}, u32[]{:S(2)}) %collective-permute-start.22) | collective-permute-done | bytes 786464 | tf_op jit(solution)/shard_map/ppermute | solution.py:571
  144.4 11.4 %collective-permute-done.15 = bf16[512,768]{1,0:T(8,128)(2,1)S(1)} collective-permute-done((bf16[512,768]{1,0:T(8,128)(2,1)S(1)}, bf16[512,768]{1,0:T(8,128)(2,1)S(1)}, u32[]{:S(2)}, u32[]{:S(2)}) %collective-permute-start.15) | collective-permute-done | bytes 786464 | tf_op jit(solution)/shard_map/ppermute | solution.py:570
  157.0 4.7 %collective-permute-done.23 = bf16[512,768]{1,0:T(8,128)(2,1)S(1)} collective-permute-done((bf16[512,768]{1,0:T(8,128)(2,1)S(1)}, bf16[512,768]{1,0:T(8,128)(2,1)S(1)}, u32[]{:S(2)}, u32[]{:S(2)}) %collective-permute-start.23) | collective-permute-done | bytes 786464 | tf_op jit(solution)/shard_map/ppermute | solution.py:571
  161.8 2.7 convolution_add_fusion.2
  164.5 10.4 %collective-permute-done.31.refs_4_ = bf16[512,4096]{1,0:T(8,128)(2,1)} collective-permute-done((bf16[512,4096]{1,0:T(8,128)(2,1)}, bf16[512,4096]{1,0:T(8,128)(2,1)}, u32[]{:S(2)}, u32[]{:S(2)}) %collective-permute-start.31) | collective-permute-done | bytes 4194336 | tf_op jit(solution)/shard_map/ppermute | solution.py:537
  175.8 2.6 convolution_add_fusion.8
  179.3 5.0 %convolution_add_fusion.1 = f32[1024,768]{1,0:T(8,128)} fusion(f32[1024,768]{1,0:T(8,128)} %convolution_add_fusion.2, bf16[512,768]{1,0:T(8,128)(2,1)S(1)} %copy-done.38, bf16[1024,4096]{1,0:T(8,128)(2,1)} %copy-done.2), kind=kOutput, calls=%fused_computation.4 | convolution fusion | flops 806092800 | bytes 8126464 | tf_op jit(solution)/shard_map/dot_general | solution.py:564
  184.3 4.0 %convolution_add_fusion.7 = f32[1024,768]{1,0:T(8,128)} fusion(f32[1024,768]{1,0:T(8,128)S(1)} %copy-done.37, bf16[512,768]{1,0:T(8,128)(2,1)S(1)} %copy-done.39, bf16[1024,4096]{1,0:T(8,128)(2,1)} %copy-done.2), kind=kOutput, calls=%fused_computation.10 | convolution fusion | flops 806092800 | bytes 8126464 | tf_op jit(solution)/shard_map/dot_general | solution.py:564
  192.4 4.1 %all-to-all-start.2 = ((bf16[32,16,512]{2,1,0:T(8,128)(2,1)}), bf16[32,16,512]{2,1,0:T(8,128)(2,1)S(1)}, u32[]{:S(2)}, u32[]{:S(2)}) async-start(bf16[32,16,512]{2,1,0:T(8,128)(2,1)} %bitcast.16), calls=%async_computation.2 | async-start | bytes 1048576 | tf_op jit(solution)/shard_map/all_to_all | solution.py:626
  196.5 2.2 collective-permute-done.24
  199.5 3.4 %convolution_add_fusion = f32[1024,768]{1,0:T(8,128)S(1)} fusion(f32[1024,768]{1,0:T(8,128)} %convolution_add_fusion.1, bf16[512,768]{1,0:T(8,128)(2,1)} %collective-permute-done.24, bf16[1024,4096]{1,0:T(8,128)(2,1)} %copy-done.2), kind=kOutput, calls=%fused_computation.3 | convolution fusion | flops 806092800 | bytes 8126464 | tf_op jit(solution)/shard_map/dot_general | solution.py:564
  202.9 6.5 %collective-permute-done.17 = bf16[512,768]{1,0:T(8,128)(2,1)} collective-permute-done((bf16[512,768]{1,0:T(8,128)(2,1)S(1)}, bf16[512,768]{1,0:T(8,128)(2,1)}, u32[]{:S(2)}, u32[]{:S(2)}) %collective-permute-start.17) | collective-permute-done | bytes 786464 | tf_op jit(solution)/shard_map/ppermute | solution.py:570
  210.3 2.4 convolution_add_fusion.6
  212.7 11.8 %collective-permute-done.25 = bf16[512,768]{1,0:T(8,128)(2,1)S(1)} collective-permute-done((bf16[512,768]{1,0:T(8,128)(2,1)}, bf16[512,768]{1,0:T(8,128)(2,1)S(1)}, u32[]{:S(2)}, u32[]{:S(2)}) %collective-permute-start.25) | collective-permute-done | bytes 786464 | tf_op jit(solution)/shard_map/ppermute | solution.py:571
  224.6 2.2 add_convert_fusion.refs_1_.refs_3_
  226.8 5.5 %collective-permute-done.18 = bf16[512,768]{1,0:T(8,128)(2,1)S(1)} collective-permute-done((bf16[512,768]{1,0:T(8,128)(2,1)}, bf16[512,768]{1,0:T(8,128)(2,1)S(1)}, u32[]{:S(2)}, u32[]{:S(2)}) %collective-permute-start.18) | collective-permute-done | bytes 786464 | tf_op jit(solution)/shard_map/ppermute | solution.py:570
  232.3 2.2 add_convert_fusion.1.refs_0_.refs_2_
  234.6 3.0 shard_map.179
  238.3 3.0 shard_map.178
  243.2 7.3 %collective-permute-done.26.refs_0_ = bf16[256,512]{1,0:T(8,128)(2,1)S(1)} collective-permute-done((bf16[256,512]{1,0:T(8,128)(2,1)S(1)}, bf16[256,512]{1,0:T(8,128)(2,1)S(1)}, u32[]{:S(2)}, u32[]{:S(2)}) %collective-permute-start.26) | collective-permute-done | bytes 262176 | tf_op jit(solution)/shard_map/ppermute | solution.py:537
  250.5 4.7 %collective-permute-done.27.refs_1_ = bf16[256,512]{1,0:T(8,128)(2,1)S(1)} collective-permute-done((bf16[256,512]{1,0:T(8,128)(2,1)S(1)}, bf16[256,512]{1,0:T(8,128)(2,1)S(1)}, u32[]{:S(2)}, u32[]{:S(2)}) %collective-permute-start.27) | collective-permute-done | bytes 262176 | tf_op jit(solution)/shard_map/ppermute | solution.py:537
  255.9 13.8 %shard_map.181 = (bf16[256,1024]{1,0:T(8,128)(2,1)}, bf16[256,1024]{1,0:T(8,128)(2,1)}, bf16[256,1024]{1,0:T(8,128)(2,1)}, bf16[256,1024]{1,0:T(8,128)(2,1)}) custom-call(s32[8]{0:T(128)} %get-tuple-element.42.step_ref, s32[1]{0:T(128)} %bitcast.group_ref, bf16[1024,4096]{1,0:T(8,128)(2,1)} %tok_ref.3, bf16[256,512]{1,0:T(8,128)(2,1)} %copy-done.46, ...), custom_call_target="tpu_custom_call" | custom-call | flops 4294967296 | bytes 20971520 | tf_op jit(solution)/shard_map/pallas_call | solution.py:294
  273.9 5.0 %shard_map.184 = bf16[32,16,640]{2,1,0:T(8,128)(2,1)} custom-call(s32[1]{0:T(128)} %bitcast.group_ref, s32[4]{0:T(128)S(1)} %copy-done.34, f32[4]{0:T(128)S(1)} %copy-done.35, f32[1,4096]{1,0:T(1,128)S(1)} %bitcast.49, bf16[32,16,512]{2,1,0:T(8,128)(2,1)S(1)} %all-to-all-done.2.folded_ref, bf16[256,1024]{1,0:T(8,128)(2,1)S(1)} %copy-done.5, ...), custom_call_target="tpu_custom_call" | custom-call | flops 402653184 | bytes 2097152 | tf_op jit(solution)/shard_map/pallas_call | solution.py:388
  278.9 7.2 %all-to-all-start.3 = ((bf16[32,16,640]{2,1,0:T(8,128)(2,1)}), bf16[32,16,640]{2,1,0:T(8,128)(2,1)S(1)}, u32[]{:S(2)}, u32[]{:S(2)}) async-start(bf16[32,16,640]{2,1,0:T(8,128)(2,1)} %shard_map.184), calls=%async_computation.3 | async-start | bytes 1310720 | tf_op jit(solution)/shard_map/all_to_all | solution.py:643
  286.4 1.6 collective-permute-start.35
  288.2 15.8 %all-to-all-done.3.got_ref = bf16[32,16,640]{2,1,0:T(8,128)(2,1)S(1)} async-done(((bf16[32,16,640]{2,1,0:T(8,128)(2,1)}), bf16[32,16,640]{2,1,0:T(8,128)(2,1)S(1)}, u32[]{:S(2)}, u32[]{:S(2)}) %all-to-all-start.3) | async-done | bytes 655392 | tf_op jit(solution)/shard_map/all_to_all | solution.py:643
  304.0 1.5 shard_map.185
  305.6 3.4 %all-to-all-start.4 = ((bf16[32,8,512]{2,1,0:T(8,128)(2,1)}), bf16[32,8,512]{2,1,0:T(8,128)(2,1)S(1)}, u32[]{:S(2)}, u32[]{:S(2)}) async-start(bf16[32,8,512]{2,1,0:T(8,128)(2,1)} %shard_map.185), calls=%async_computation.4 | async-start | bytes 524288 | tf_op jit(solution)/shard_map/all_to_all | solution.py:648
  310.5 1.6 collective-permute-start.38
  312.2 8.2 %collective-permute-done.36.refs_3_ = bf16[256,1024]{1,0:T(8,128)(2,1)} collective-permute-done((bf16[256,1024]{1,0:T(8,128)(2,1)S(1)}, bf16[256,1024]{1,0:T(8,128)(2,1)}, u32[]{:S(2)}, u32[]{:S(2)}) %collective-permute-start.36) | collective-permute-done | bytes 524320 | tf_op jit(solution)/shard_map/ppermute | solution.py:537
  320.3 3.2 shard_map.182
  324.6 1.7 collective-permute-done.39.refs_3_
  (202 shorter events, 50.4 us)
Async XLA Ops:
  0.6 88.2 %copy-start = (bf16[512,512]{1,0:T(8,128)(2,1)S(1)}, bf16[512,512]{1,0:T(8,128)(2,1)}, u32[]{:S(2)}) copy-start(bf16[512,512]{1,0:T(8,128)(2,1)} %param.29) | copy-start | bytes 1572868
  1.8 12.2 %collective-permute-start.6 = (bf16[256,512]{1,0:T(8,128)(2,1)S(1)}, bf16[256,512]{1,0:T(8,128)(2,1)S(1)}, u32[]{:S(2)}, u32[]{:S(2)}) collective-permute-start(bf16[256,512]{1,0:T(8,128)(2,1)S(1)} %get-tuple-element.33.refs_8_), channel_id=1, source_target_pairs={{8,0},{16,8},{24,16},{28,24},{20,28},{12,20},{4,12},{0,4},{9,1},{1... | collective-permute-start | bytes 786440 | tf_op jit(solution)/shard_map/ppermute | solution.py:547
  4.8 11.1 %collective-permute-start = (bf16[256,512]{1,0:T(8,128)(2,1)S(1)}, bf16[256,512]{1,0:T(8,128)(2,1)S(1)}, u32[]{:S(2)}, u32[]{:S(2)}) collective-permute-start(bf16[256,512]{1,0:T(8,128)(2,1)S(1)} %get-tuple-element.34.refs_0_), channel_id=1, source_target_pairs={{0,8},{8,16},{16,24},{24,28},{28,20},{20,12},{12,4},{4,0},{1,9},{9... | collective-permute-start | bytes 786440 | tf_op jit(solution)/shard_map/ppermute | solution.py:546
  10.7 61.1 %all-to-all-start = ((bf16[4,8,512]{2,1,0:T(8,128)(2,1)}), bf16[4,8,512]{2,1,0:T(8,128)(2,1)S(1)}, u32[]{:S(2)}, u32[]{:S(2)}) async-start(bf16[4,8,512]{2,1,0:T(8,128)(2,1)} %broadcast_in_dim.8), calls=%async_computation | async-start | bytes 65536 | tf_op jit(solution)/shard_map/all_to_all | solution.py:589
  13.9 8.9 %collective-permute-start.7 = (bf16[256,512]{1,0:T(8,128)(2,1)S(1)}, bf16[256,512]{1,0:T(8,128)(2,1)S(1)}, u32[]{:S(2)}, u32[]{:S(2)}) collective-permute-start(bf16[256,512]{1,0:T(8,128)(2,1)S(1)} %collective-permute-done.6.refs_15_), channel_id=1, source_target_pairs={{8,0},{16,8},{24,16},{28,24},{20,28},{12,20},{4,12},{0,4},{9,1},{1... | collective-permute-start | bytes 786440 | tf_op jit(solution)/shard_map/ppermute | solution.py:547
  15.9 17.0 %copy-start.14 = (bf16[256,512]{1,0:T(8,128)(2,1)}, bf16[256,512]{1,0:T(8,128)(2,1)S(1)}, u32[]{:S(2)}) copy-start(bf16[256,512]{1,0:T(8,128)(2,1)S(1)} %collective-permute-done.refs_1_) | copy-start | bytes 786436
  15.9 8.6 %collective-permute-start.1 = (bf16[256,512]{1,0:T(8,128)(2,1)S(1)}, bf16[256,512]{1,0:T(8,128)(2,1)S(1)}, u32[]{:S(2)}, u32[]{:S(2)}) collective-permute-start(bf16[256,512]{1,0:T(8,128)(2,1)S(1)} %collective-permute-done.refs_1_), channel_id=1, source_target_pairs={{0,8},{8,16},{16,24},{24,28},{28,20},{20,12},{12,4},{4,0},{1,9},{9... | collective-permute-start | bytes 786440 | tf_op jit(solution)/shard_map/ppermute | solution.py:546
  22.8 18.1 %copy-start.16 = (bf16[256,512]{1,0:T(8,128)(2,1)}, bf16[256,512]{1,0:T(8,128)(2,1)S(1)}, u32[]{:S(2)}) copy-start(bf16[256,512]{1,0:T(8,128)(2,1)S(1)} %collective-permute-done.7.refs_14_) | copy-start | bytes 786436
  22.8 8.0 %collective-permute-start.8 = (bf16[256,512]{1,0:T(8,128)(2,1)S(1)}, bf16[256,512]{1,0:T(8,128)(2,1)S(1)}, u32[]{:S(2)}, u32[]{:S(2)}) collective-permute-start(bf16[256,512]{1,0:T(8,128)(2,1)S(1)} %collective-permute-done.7.refs_14_), channel_id=1, source_target_pairs={{8,0},{16,8},{24,16},{28,24},{20,28},{12,20},{4,12},{0,4},{9,1},{1... | collective-permute-start | bytes 786440 | tf_op jit(solution)/shard_map/ppermute | solution.py:547
  24.5 16.4 %copy-start.18 = (bf16[256,512]{1,0:T(8,128)(2,1)}, bf16[256,512]{1,0:T(8,128)(2,1)S(1)}, u32[]{:S(2)}) copy-start(bf16[256,512]{1,0:T(8,128)(2,1)S(1)} %collective-permute-done.1.refs_2_) | copy-start | bytes 786436
  24.5 7.8 %collective-permute-start.2 = (bf16[256,512]{1,0:T(8,128)(2,1)S(1)}, bf16[256,512]{1,0:T(8,128)(2,1)S(1)}, u32[]{:S(2)}, u32[]{:S(2)}) collective-permute-start(bf16[256,512]{1,0:T(8,128)(2,1)S(1)} %collective-permute-done.1.refs_2_), channel_id=1, source_target_pairs={{0,8},{8,16},{16,24},{24,28},{28,20},{20,12},{12,4},{4,0},{1,9},{9... | collective-permute-start | bytes 786440 | tf_op jit(solution)/shard_map/ppermute | solution.py:546
  24.9 16.1 %copy-start.48 = (f32[32,512]{1,0:T(8,128)S(1)}, f32[32,512]{1,0:T(8,128)}, u32[]{:S(2)}) copy-start(f32[32,512]{1,0:T(8,128)} %constant.45.clone) | copy-start | bytes 196612
  24.9 16.1 %copy-start.49 = (f32[8,32]{1,0:T(8,128)S(1)}, f32[8,32]{1,0:T(8,128)}, u32[]{:S(2)}) copy-start(f32[8,32]{1,0:T(8,128)} %param.23) | copy-start | bytes 3076
  30.8 18.9 %copy-start.20 = (bf16[256,512]{1,0:T(8,128)(2,1)}, bf16[256,512]{1,0:T(8,128)(2,1)S(1)}, u32[]{:S(2)}) copy-start(bf16[256,512]{1,0:T(8,128)(2,1)S(1)} %collective-permute-done.8.refs_13_) | copy-start | bytes 786436
  30.8 7.1 %collective-permute-start.9 = (bf16[256,512]{1,0:T(8,128)(2,1)S(1)}, bf16[256,512]{1,0:T(8,128)(2,1)S(1)}, u32[]{:S(2)}, u32[]{:S(2)}) collective-permute-start(bf16[256,512]{1,0:T(8,128)(2,1)S(1)} %collective-permute-done.8.refs_13_), channel_id=1, source_target_pairs={{8,0},{16,8},{24,16},{28,24},{20,28},{12,20},{4,12},{0,4},{9,1},{1... | collective-permute-start | bytes 786440 | tf_op jit(solution)/shard_map/ppermute | solution.py:547
  32.3 17.5 %copy-start.22 = (bf16[256,512]{1,0:T(8,128)(2,1)}, bf16[256,512]{1,0:T(8,128)(2,1)S(1)}, u32[]{:S(2)}) copy-start(bf16[256,512]{1,0:T(8,128)(2,1)S(1)} %collective-permute-done.2.refs_3_) | copy-start | bytes 786436
  32.3 6.9 %collective-permute-start.3 = (bf16[256,512]{1,0:T(8,128)(2,1)S(1)}, bf16[256,512]{1,0:T(8,128)(2,1)S(1)}, u32[]{:S(2)}, u32[]{:S(2)}) collective-permute-start(bf16[256,512]{1,0:T(8,128)(2,1)S(1)} %collective-permute-done.2.refs_3_), channel_id=1, source_target_pairs={{0,8},{8,16},{16,24},{24,28},{28,20},{20,12},{12,4},{4,0},{1,9},{9... | collective-permute-start | bytes 786440 | tf_op jit(solution)/shard_map/ppermute | solution.py:546
  33.9 24.7 %copy-start.51 = (s32[4]{0:T(128)S(1)}, s32[4]{0:T(128)}, u32[]{:S(2)}) copy-start(s32[4]{0:T(128)} %param.19) | copy-start | bytes 52
  37.9 19.4 %copy-start.24 = (bf16[256,512]{1,0:T(8,128)(2,1)}, bf16[256,512]{1,0:T(8,128)(2,1)S(1)}, u32[]{:S(2)}) copy-start(bf16[256,512]{1,0:T(8,128)(2,1)S(1)} %collective-permute-done.9.refs_12_) | copy-start | bytes 786436
  37.9 6.9 %collective-permute-start.10 = (bf16[256,512]{1,0:T(8,128)(2,1)S(1)}, bf16[256,512]{1,0:T(8,128)(2,1)S(1)}, u32[]{:S(2)}, u32[]{:S(2)}) collective-permute-start(bf16[256,512]{1,0:T(8,128)(2,1)S(1)} %collective-permute-done.9.refs_12_), channel_id=1, source_target_pairs={{8,0},{16,8},{24,16},{28,24},{20,28},{12,20},{4,12},{0,4},{9,1},{1... | collective-permute-start | bytes 786440 | tf_op jit(solution)/shard_map/ppermute | solution.py:547
  39.2 18.2 %copy-start.26 = (bf16[256,512]{1,0:T(8,128)(2,1)}, bf16[256,512]{1,0:T(8,128)(2,1)S(1)}, u32[]{:S(2)}) copy-start(bf16[256,512]{1,0:T(8,128)(2,1)S(1)} %collective-permute-done.3.refs_4_) | copy-start | bytes 786436
  39.2 7.1 %collective-permute-start.4 = (bf16[256,512]{1,0:T(8,128)(2,1)S(1)}, bf16[256,512]{1,0:T(8,128)(2,1)S(1)}, u32[]{:S(2)}, u32[]{:S(2)}) collective-permute-start(bf16[256,512]{1,0:T(8,128)(2,1)S(1)} %collective-permute-done.3.refs_4_), channel_id=1, source_target_pairs={{0,8},{8,16},{16,24},{24,28},{28,20},{20,12},{12,4},{4,0},{1,9},{9... | collective-permute-start | bytes 786440 | tf_op jit(solution)/shard_map/ppermute | solution.py:546
  40.0 20.7 %copy-start.33 = (f32[4096]{0:T(1024)S(1)}, f32[4096]{0:T(1024)}, u32[]{:S(2)}) copy-start(f32[4096]{0:T(1024)} %param.21) | copy-start | bytes 49156
  44.8 6.6 %collective-permute-start.11 = (bf16[256,512]{1,0:T(8,128)(2,1)S(1)}, bf16[256,512]{1,0:T(8,128)(2,1)}, u32[]{:S(2)}, u32[]{:S(2)}) collective-permute-start(bf16[256,512]{1,0:T(8,128)(2,1)S(1)} %collective-permute-done.10.refs_11_), channel_id=1, source_target_pairs={{8,0},{16,8},{24,16},{28,24},{20,28},{12,20},{4,12},{0,4},{9,1},{1... | collective-permute-start | bytes 786440 | tf_op jit(solution)/shard_map/ppermute | solution.py:547
  46.3 6.5 %collective-permute-start.5 = (bf16[256,512]{1,0:T(8,128)(2,1)S(1)}, bf16[256,512]{1,0:T(8,128)(2,1)}, u32[]{:S(2)}, u32[]{:S(2)}) collective-permute-start(bf16[256,512]{1,0:T(8,128)(2,1)S(1)} %collective-permute-done.4.refs_5_), channel_id=1, source_target_pairs={{0,8},{8,16},{16,24},{24,28},{28,20},{20,12},{12,4},{4,0},{1,9},{9... | collective-permute-start | bytes 786440 | tf_op jit(solution)/shard_map/ppermute | solution.py:546
  52.7 36.4 %collective-permute-start.19 = (bf16[512,768]{1,0:T(8,128)(2,1)}, bf16[512,768]{1,0:T(8,128)(2,1)}, u32[]{:S(2)}, u32[]{:S(2)}) collective-permute-start(bf16[512,768]{1,0:T(8,128)(2,1)} %pad_maximum_fusion.1), channel_id=1, source_target_pairs={{8,0},{16,8},{24,16},{28,24},{20,28},{12,20},{4,12},{0,4},{9,1},{1... | collective-permute-start | bytes 2359304 | tf_op jit(solution)/shard_map/ppermute | solution.py:571
  54.3 41.3 %collective-permute-start.12 = (bf16[512,768]{1,0:T(8,128)(2,1)}, bf16[512,768]{1,0:T(8,128)(2,1)}, u32[]{:S(2)}, u32[]{:S(2)}) collective-permute-start(bf16[512,768]{1,0:T(8,128)(2,1)} %pad_maximum_fusion), channel_id=1, source_target_pairs={{0,8},{8,16},{16,24},{24,28},{28,20},{20,12},{12,4},{4,0},{1,9},{9... | collective-permute-start | bytes 2359304 | tf_op jit(solution)/shard_map/ppermute | solution.py:570
  54.8 20.5 %collective-permute-start.29 = (bf16[256,512]{1,0:T(8,128)(2,1)}, bf16[256,512]{1,0:T(8,128)(2,1)}, u32[]{:S(2)}, u32[]{:S(2)}) collective-permute-start(bf16[256,512]{1,0:T(8,128)(2,1)} %collective-permute-done.5.refs_6_), channel_id=1, source_target_pairs={{0,8},{8,16},{16,24},{24,28},{28,20},{20,12},{12,4},{4,0},{1,9},{9... | collective-permute-start | bytes 786440 | tf_op jit(solution)/shard_map/ppermute | solution.py:546
  56.5 18.7 %collective-permute-start.30 = (bf16[256,512]{1,0:T(8,128)(2,1)}, bf16[256,512]{1,0:T(8,128)(2,1)}, u32[]{:S(2)}, u32[]{:S(2)}) collective-permute-start(bf16[256,512]{1,0:T(8,128)(2,1)} %collective-permute-done.11.refs_10_), channel_id=1, source_target_pairs={{8,0},{16,8},{24,16},{28,24},{20,28},{12,20},{4,12},{0,4},{9,1},{1... | collective-permute-start | bytes 786440 | tf_op jit(solution)/shard_map/ppermute | solution.py:547
  71.7 17.1 %copy-start.50 = (f32[512]{0:T(512)S(1)}, f32[512]{0:T(512)}, u32[]{:S(2)}) copy-start(f32[512]{0:T(512)} %param.28) | copy-start | bytes 6148
  87.4 87.5 %collective-permute-start.31 = (bf16[512,4096]{1,0:T(8,128)(2,1)}, bf16[512,4096]{1,0:T(8,128)(2,1)}, u32[]{:S(2)}, u32[]{:S(2)}) collective-permute-start(bf16[512,4096]{1,0:T(8,128)(2,1)} %shard_map.180.refs_7_), channel_id=1, source_target_pairs={{0,2},{1,3},{2,0},{3,1},{4,6},{5,7},{6,4},{7,5},{8,10},{9,11},{10,... | collective-permute-start | bytes 12582920 | tf_op jit(solution)/shard_map/ppermute | solution.py:537
  89.2 15.6 %collective-permute-start.20 = (bf16[512,768]{1,0:T(8,128)(2,1)}, bf16[512,768]{1,0:T(8,128)(2,1)S(1)}, u32[]{:S(2)}, u32[]{:S(2)}) collective-permute-start(bf16[512,768]{1,0:T(8,128)(2,1)} %collective-permute-done.19), channel_id=1, source_target_pairs={{8,0},{16,8},{24,16},{28,24},{20,28},{12,20},{4,12},{0,4},{9,1},{1... | collective-permute-start | bytes 2359304 | tf_op jit(solution)/shard_map/ppermute | solution.py:571
  91.5 86.9 %all-to-all-start.1 = ((f32[8,16,512]{2,1,0:T(8,128)}), f32[8,16,512]{2,1,0:T(8,128)S(1)}, u32[]{:S(2)}, u32[]{:S(2)}) async-start(f32[8,16,512]{2,1,0:T(8,128)} %broadcast_in_dim.10), calls=%async_computation.1 | async-start | bytes 524288 | tf_op jit(solution)/shard_map/all_to_all | solution.py:608
  95.6 147.6 %collective-permute-start.33 = (bf16[512,4096]{1,0:T(8,128)(2,1)}, bf16[512,4096]{1,0:T(8,128)(2,1)}, u32[]{:S(2)}, u32[]{:S(2)}) collective-permute-start(bf16[512,4096]{1,0:T(8,128)(2,1)} %shard_map.180.refs_7_), channel_id=1, source_target_pairs={{0,1},{1,0},{2,3},{3,2},{4,5},{5,4},{6,7},{7,6},{8,9},{9,8},{10,11... | collective-permute-start | bytes 12582920 | tf_op jit(solution)/shard_map/ppermute | solution.py:537
  95.7 21.8 %collective-permute-start.13 = (bf16[512,768]{1,0:T(8,128)(2,1)}, bf16[512,768]{1,0:T(8,128)(2,1)S(1)}, u32[]{:S(2)}, u32[]{:S(2)}) collective-permute-start(bf16[512,768]{1,0:T(8,128)(2,1)} %collective-permute-done.12), channel_id=1, source_target_pairs={{0,8},{8,16},{16,24},{24,28},{28,20},{20,12},{12,4},{4,0},{1,9},{9... | collective-permute-start | bytes 2359304 | tf_op jit(solution)/shard_map/ppermute | solution.py:570
  104.8 19.2 %collective-permute-start.21 = (bf16[512,768]{1,0:T(8,128)(2,1)S(1)}, bf16[512,768]{1,0:T(8,128)(2,1)S(1)}, u32[]{:S(2)}, u32[]{:S(2)}) collective-permute-start(bf16[512,768]{1,0:T(8,128)(2,1)S(1)} %collective-permute-done.20), channel_id=1, source_target_pairs={{8,0},{16,8},{24,16},{28,24},{20,28},{12,20},{4,12},{0,4},{9,1},{1... | collective-permute-start | bytes 2359304 | tf_op jit(solution)/shard_map/ppermute | solution.py:571
  117.5 19.7 %collective-permute-start.14 = (bf16[512,768]{1,0:T(8,128)(2,1)S(1)}, bf16[512,768]{1,0:T(8,128)(2,1)S(1)}, u32[]{:S(2)}, u32[]{:S(2)}) collective-permute-start(bf16[512,768]{1,0:T(8,128)(2,1)S(1)} %collective-permute-done.13), channel_id=1, source_target_pairs={{0,8},{8,16},{16,24},{24,28},{28,20},{20,12},{12,4},{4,0},{1,9},{9... | collective-permute-start | bytes 2359304 | tf_op jit(solution)/shard_map/ppermute | solution.py:570
  124.0 19.4 %collective-permute-start.22 = (bf16[512,768]{1,0:T(8,128)(2,1)S(1)}, bf16[512,768]{1,0:T(8,128)(2,1)S(1)}, u32[]{:S(2)}, u32[]{:S(2)}) collective-permute-start(bf16[512,768]{1,0:T(8,128)(2,1)S(1)} %collective-permute-done.21), channel_id=1, source_target_pairs={{8,0},{16,8},{24,16},{28,24},{20,28},{12,20},{4,12},{0,4},{9,1},{1... | collective-permute-start | bytes 2359304 | tf_op jit(solution)/shard_map/ppermute | solution.py:571
  137.2 18.6 %collective-permute-start.15 = (bf16[512,768]{1,0:T(8,128)(2,1)S(1)}, bf16[512,768]{1,0:T(8,128)(2,1)S(1)}, u32[]{:S(2)}, u32[]{:S(2)}) collective-permute-start(bf16[512,768]{1,0:T(8,128)(2,1)S(1)} %collective-permute-done.14), channel_id=1, source_target_pairs={{0,8},{8,16},{16,24},{24,28},{28,20},{20,12},{12,4},{4,0},{1,9},{9... | collective-permute-start | bytes 2359304 | tf_op jit(solution)/shard_map/ppermute | solution.py:570
  143.4 18.4 %collective-permute-start.23 = (bf16[512,768]{1,0:T(8,128)(2,1)S(1)}, bf16[512,768]{1,0:T(8,128)(2,1)S(1)}, u32[]{:S(2)}, u32[]{:S(2)}) collective-permute-start(bf16[512,768]{1,0:T(8,128)(2,1)S(1)} %collective-permute-done.22), channel_id=1, source_target_pairs={{8,0},{16,8},{24,16},{28,24},{20,28},{12,20},{4,12},{0,4},{9,1},{1... | collective-permute-start | bytes 2359304 | tf_op jit(solution)/shard_map/ppermute | solution.py:571
  155.8 19.1 %collective-permute-start.16 = (bf16[512,768]{1,0:T(8,128)(2,1)S(1)}, bf16[512,768]{1,0:T(8,128)(2,1)S(1)}, u32[]{:S(2)}, u32[]{:S(2)}) collective-permute-start(bf16[512,768]{1,0:T(8,128)(2,1)S(1)} %collective-permute-done.15), channel_id=1, source_target_pairs={{0,8},{8,16},{16,24},{24,28},{28,20},{20,12},{12,4},{4,0},{1,9},{9... | collective-permute-start | bytes 2359304 | tf_op jit(solution)/shard_map/ppermute | solution.py:570
  164.5 14.8 %copy-start.38 = (bf16[512,768]{1,0:T(8,128)(2,1)S(1)}, bf16[512,768]{1,0:T(8,128)(2,1)}, u32[]{:S(2)}) copy-start(bf16[512,768]{1,0:T(8,128)(2,1)} %pad_maximum_fusion.1) | copy-start | bytes 2359300
  174.9 80.3 %collective-permute-start.32 = (bf16[512,4096]{1,0:T(8,128)(2,1)}, bf16[512,4096]{1,0:T(8,128)(2,1)}, u32[]{:S(2)}, u32[]{:S(2)}) collective-permute-start(bf16[512,4096]{1,0:T(8,128)(2,1)} %collective-permute-done.31.refs_4_), channel_id=1, source_target_pairs={{0,1},{1,0},{2,3},{3,2},{4,5},{5,4},{6,7},{7,6},{8,9},{9,8},{10,11... | collective-permute-start | bytes 12582920 | tf_op jit(solution)/shard_map/ppermute | solution.py:537
  178.4 20.3 %collective-permute-start.24 = (bf16[512,768]{1,0:T(8,128)(2,1)}, bf16[512,768]{1,0:T(8,128)(2,1)}, u32[]{:S(2)}, u32[]{:S(2)}) collective-permute-start(bf16[512,768]{1,0:T(8,128)(2,1)} %copy-done.42), channel_id=1, source_target_pairs={{8,0},{16,8},{24,16},{28,24},{20,28},{12,20},{4,12},{0,4},{9,1},{1... | collective-permute-start | bytes 2359304 | tf_op jit(solution)/shard_map/ppermute | solution.py:571
  188.5 20.9 %collective-permute-start.17 = (bf16[512,768]{1,0:T(8,128)(2,1)S(1)}, bf16[512,768]{1,0:T(8,128)(2,1)}, u32[]{:S(2)}, u32[]{:S(2)}) collective-permute-start(bf16[512,768]{1,0:T(8,128)(2,1)S(1)} %copy-done.44), channel_id=1, source_target_pairs={{0,8},{8,16},{16,24},{24,28},{28,20},{20,12},{12,4},{4,0},{1,9},{9... | collective-permute-start | bytes 2359304 | tf_op jit(solution)/shard_map/ppermute | solution.py:570
  192.4 77.3 %all-to-all-start.2 = ((bf16[32,16,512]{2,1,0:T(8,128)(2,1)}), bf16[32,16,512]{2,1,0:T(8,128)(2,1)S(1)}, u32[]{:S(2)}, u32[]{:S(2)}) async-start(bf16[32,16,512]{2,1,0:T(8,128)(2,1)} %bitcast.16), calls=%async_computation.2 | async-start | bytes 1048576 | tf_op jit(solution)/shard_map/all_to_all | solution.py:626
  196.5 13.8 %copy-start.36 = (f32[1024,768]{1,0:T(8,128)S(1)}, f32[1024,768]{1,0:T(8,128)}, u32[]{:S(2)}) copy-start(f32[1024,768]{1,0:T(8,128)} %convolution_add_fusion.7) | copy-start | bytes 9437188
  198.7 25.9 %collective-permute-start.25 = (bf16[512,768]{1,0:T(8,128)(2,1)}, bf16[512,768]{1,0:T(8,128)(2,1)S(1)}, u32[]{:S(2)}, u32[]{:S(2)}) collective-permute-start(bf16[512,768]{1,0:T(8,128)(2,1)} %collective-permute-done.24), channel_id=1, source_target_pairs={{8,0},{16,8},{24,16},{28,24},{20,28},{12,20},{4,12},{0,4},{9,1},{1... | collective-permute-start | bytes 2359304 | tf_op jit(solution)/shard_map/ppermute | solution.py:571
  209.3 23.0 %collective-permute-start.18 = (bf16[512,768]{1,0:T(8,128)(2,1)}, bf16[512,768]{1,0:T(8,128)(2,1)S(1)}, u32[]{:S(2)}, u32[]{:S(2)}) collective-permute-start(bf16[512,768]{1,0:T(8,128)(2,1)} %collective-permute-done.17), channel_id=1, source_target_pairs={{0,8},{8,16},{16,24},{24,28},{28,20},{20,12},{12,4},{4,0},{1,9},{9... | collective-permute-start | bytes 2359304 | tf_op jit(solution)/shard_map/ppermute | solution.py:570
  238.3 4.9 %collective-permute-start.28 = (bf16[256,512]{1,0:T(8,128)(2,1)S(1)}, bf16[256,512]{1,0:T(8,128)(2,1)S(1)}, u32[]{:S(2)}, u32[]{:S(2)}) collective-permute-start(bf16[256,512]{1,0:T(8,128)(2,1)S(1)} %get-tuple-element.17), channel_id=1, source_target_pairs={{0,1},{1,0},{2,3},{3,2},{4,5},{5,4},{6,7},{7,6},{8,9},{9,8},{10,11... | collective-permute-start | bytes 786440 | tf_op jit(solution)/shard_map/ppermute | solution.py:537
  241.3 9.2 %collective-permute-start.26 = (bf16[256,512]{1,0:T(8,128)(2,1)S(1)}, bf16[256,512]{1,0:T(8,128)(2,1)S(1)}, u32[]{:S(2)}, u32[]{:S(2)}) collective-permute-start(bf16[256,512]{1,0:T(8,128)(2,1)S(1)} %get-tuple-element.15), channel_id=1, source_target_pairs={{0,2},{1,3},{2,0},{3,1},{4,6},{5,7},{6,4},{7,5},{8,10},{9,11},{10,... | collective-permute-start | bytes 786440 | tf_op jit(solution)/shard_map/ppermute | solution.py:537
  242.1 13.2 %collective-permute-start.27 = (bf16[256,512]{1,0:T(8,128)(2,1)S(1)}, bf16[256,512]{1,0:T(8,128)(2,1)S(1)}, u32[]{:S(2)}, u32[]{:S(2)}) collective-permute-start(bf16[256,512]{1,0:T(8,128)(2,1)S(1)} %get-tuple-element.16), channel_id=1, source_target_pairs={{0,3},{1,2},{2,1},{3,0},{4,7},{5,6},{6,5},{7,4},{8,11},{9,10},{10,... | collective-permute-start | bytes 786440 | tf_op jit(solution)/shard_map/ppermute | solution.py:537
  255.9 48.1 %copy-start.7 = (bf16[512,512]{1,0:T(8,128)(2,1)S(1)}, bf16[512,512]{1,0:T(8,128)(2,1)}, u32[]{:S(2)}) copy-start(bf16[512,512]{1,0:T(8,128)(2,1)} %get-tuple-element.27.weight_ref) | copy-start | bytes 1572868
  273.9 14.1 %copy-start.9 = (bf16[256,1024]{1,0:T(8,128)(2,1)S(1)}, bf16[256,1024]{1,0:T(8,128)(2,1)}, u32[]{:S(2)}) copy-start(bf16[256,1024]{1,0:T(8,128)(2,1)} %get-tuple-element.22.refs_3_) | copy-start | bytes 1572868
  273.9 46.5 %copy-start.6 = (bf16[256,1024]{1,0:T(8,128)(2,1)S(1)}, bf16[256,1024]{1,0:T(8,128)(2,1)}, u32[]{:S(2)}) copy-start(bf16[256,1024]{1,0:T(8,128)(2,1)} %get-tuple-element.19.refs_0_) | copy-start | bytes 1572868
  278.9 25.2 %all-to-all-start.3 = ((bf16[32,16,640]{2,1,0:T(8,128)(2,1)}), bf16[32,16,640]{2,1,0:T(8,128)(2,1)S(1)}, u32[]{:S(2)}, u32[]{:S(2)}) async-start(bf16[32,16,640]{2,1,0:T(8,128)(2,1)} %shard_map.184), calls=%async_computation.3 | async-start | bytes 1310720 | tf_op jit(solution)/shard_map/all_to_all | solution.py:643
  286.0 26.1 %collective-permute-start.34 = (bf16[256,1024]{1,0:T(8,128)(2,1)}, bf16[256,1024]{1,0:T(8,128)(2,1)}, u32[]{:S(2)}, u32[]{:S(2)}) collective-permute-start(bf16[256,1024]{1,0:T(8,128)(2,1)} %get-tuple-element.20.refs_1_), channel_id=1, source_target_pairs={{0,1},{1,0},{2,3},{3,2},{4,5},{5,4},{6,7},{7,6},{8,9},{9,8},{10,11... | collective-permute-start | bytes 1572872 | tf_op jit(solution)/shard_map/ppermute | solution.py:537
  286.4 25.8 %collective-permute-start.35 = (bf16[256,1024]{1,0:T(8,128)(2,1)S(1)}, bf16[256,1024]{1,0:T(8,128)(2,1)}, u32[]{:S(2)}, u32[]{:S(2)}) collective-permute-start(bf16[256,1024]{1,0:T(8,128)(2,1)S(1)} %copy-done.11), channel_id=1, source_target_pairs={{0,2},{1,3},{2,0},{3,1},{4,6},{5,7},{6,4},{7,5},{8,10},{9,11},{10,... | collective-permute-start | bytes 1572872 | tf_op jit(solution)/shard_map/ppermute | solution.py:537
  288.0 32.3 %collective-permute-start.36 = (bf16[256,1024]{1,0:T(8,128)(2,1)S(1)}, bf16[256,1024]{1,0:T(8,128)(2,1)}, u32[]{:S(2)}, u32[]{:S(2)}) collective-permute-start(bf16[256,1024]{1,0:T(8,128)(2,1)S(1)} %copy-done.9), channel_id=1, source_target_pairs={{0,3},{1,2},{2,1},{3,0},{4,7},{5,6},{6,5},{7,4},{8,11},{9,10},{10,... | collective-permute-start | bytes 1572872 | tf_op jit(solution)/shard_map/ppermute | solution.py:537
  305.6 20.7 %all-to-all-start.4 = ((bf16[32,8,512]{2,1,0:T(8,128)(2,1)}), bf16[32,8,512]{2,1,0:T(8,128)(2,1)S(1)}, u32[]{:S(2)}, u32[]{:S(2)}) async-start(bf16[32,8,512]{2,1,0:T(8,128)(2,1)} %shard_map.185), calls=%async_computation.4 | async-start | bytes 524288 | tf_op jit(solution)/shard_map/all_to_all | solution.py:648
  309.0 18.1 %copy-start.1 = (bf16[512,512]{1,0:T(8,128)(2,1)S(1)}, bf16[512,512]{1,0:T(8,128)(2,1)}, u32[]{:S(2)}) copy-start(bf16[512,512]{1,0:T(8,128)(2,1)} %param.29) | copy-start | bytes 1572868
  310.2 13.3 %collective-permute-start.37 = (bf16[512,128]{1,0:T(8,128)(2,1)S(1)}, bf16[512,128]{1,0:T(8,128)(2,1)S(1)}, u32[]{:S(2)}, u32[]{:S(2)}) collective-permute-start(bf16[512,128]{1,0:T(8,128)(2,1)S(1)} %get-tuple-element.30), channel_id=1, source_target_pairs={{0,1},{1,0},{2,3},{3,2},{4,5},{5,4},{6,7},{7,6},{8,9},{9,8},{10,11... | collective-permute-start | bytes 393224 | tf_op jit(solution)/shard_map/ppermute | solution.py:537
  310.5 14.0 %collective-permute-start.38 = (bf16[512,128]{1,0:T(8,128)(2,1)S(1)}, bf16[512,128]{1,0:T(8,128)(2,1)S(1)}, u32[]{:S(2)}, u32[]{:S(2)}) collective-permute-start(bf16[512,128]{1,0:T(8,128)(2,1)S(1)} %get-tuple-element.32), channel_id=1, source_target_pairs={{0,2},{1,3},{2,0},{3,1},{4,6},{5,7},{6,4},{7,5},{8,10},{9,11},{10,... | collective-permute-start | bytes 393224 | tf_op jit(solution)/shard_map/ppermute | solution.py:537
  312.2 14.0 %collective-permute-start.39 = (bf16[512,128]{1,0:T(8,128)(2,1)S(1)}, bf16[512,128]{1,0:T(8,128)(2,1)S(1)}, u32[]{:S(2)}, u32[]{:S(2)}) collective-permute-start(bf16[512,128]{1,0:T(8,128)(2,1)S(1)} %get-tuple-element.29), channel_id=1, source_target_pairs={{0,3},{1,2},{2,1},{3,0},{4,7},{5,6},{6,5},{7,4},{8,11},{9,10},{10,... | collective-permute-start | bytes 393224 | tf_op jit(solution)/shard_map/ppermute | solution.py:537
  (35 other events, 148.7 us)
